TPU v7x, 32 devices: a whole 2x2x4 slice. The times are simulated.
32 devices in a mesh: groups: 2 (over y), tm: 16 (over z, x, core), rows: 1.
Axes of the slice: x: 2, y: 2, z: 4, core: 2. Of those that a mesh axis runs over, the one named last changes fastest.
Arguments:
- frames: bfloat16 [64, 1, 160, 384], P(('groups', 'tm'), 'rows'), parts along dimension 0, may hold values from -6 to 6
- segment_ids: int32 [64], P('groups'), parts along dimension 0, may hold values from 0 to 3, never falling along the last dimension, each value on 1 to 16 neighbouring positions
- norm_gain: float32 [384], replicated, may hold values from 0.25 to 1.75
- conv_weight: bfloat16 [384, 3, 3, 3, 384], P('tm'), may hold values from -0.0625 to 0.0625
- attn_gain: float32 [384], replicated, may hold values from 0.25 to 1.75
- w_qkv: bfloat16 [384, 1152], replicated
- w_out: bfloat16 [384, 384], replicated, may hold values from -2.5 to 2.5
Outputs:
- summed: bfloat16 [64, 1, 160, 384], P(('groups', 'tm'), 'rows'), parts along dimension 0
- attended: bfloat16 [64, 1, 160, 384], P(('groups', 'tm'), 'rows'), parts along dimension 0
There are 2 independent parts, one for each index of `groups`. A program takes and returns all parts, laid end to end along the dimension named above; an argument that names none is the same for every part. Nothing has to cross between parts.
Inputs may be any that keep to these rules, and one draw needn't show every extreme that they name: `segment_ids`: frames of one video are consecutive and ids never fall along the frames; every video has 1 to 16 frames and one has exactly 16.
All inputs are finite; a program needn't handle non-finite values.
Results may differ from a plain program's by a relative error of at most 0.013.
Values may be sent and summed in bfloat16 or wider, within the bound.
A program may use at most 64 MiB of HBM per device.

v0:
```python
import jax
import jax.numpy as jnp
from jax import lax
from jax.sharding import PartitionSpec as P

C = 384


EPSILON = 1e-06


def passed_along(value, axis, steps):
    count = lax.axis_size(axis)
    leading, last = (max(0, -steps), min(count, count - steps))
    return lax.ppermute(value, axis, [(source, source + steps) for source in range(leading, last)])


def with_halo(cells, sides, width):
    for axis, dim in sides:
        count = lax.axis_size(axis)
        ends = count - 1
        head = lax.slice_in_dim(cells, 0, width, axis=dim)
        tail = lax.slice_in_dim(cells, cells.shape[dim] - width, cells.shape[dim], axis=dim)
        cells = jnp.concatenate(
            [
                lax.ppermute(tail, axis, [(i, (i + 1) % count) for i in range(ends)]),
                cells,
                lax.ppermute(head, axis, [((i + 1) % count, i) for i in range(ends)]),
            ],
            axis=dim,
        )
    return cells


def normalize(values, gain):
    mean_square = jnp.mean(values * values, axis=-1, keepdims=True)
    return values * lax.rsqrt(mean_square + EPSILON) * gain


def absorb(carry, queries, keys, values):
    running_max, running_sum, running_acc = carry
    scores = jnp.einsum("fqc,fkc->fqk", queries, keys, preferred_element_type=jnp.float32) * C ** (
        -0.5
    )
    new_max = jnp.maximum(running_max, jnp.max(scores, axis=-1))
    expo = jnp.exp(scores - new_max[:, :, None])
    new_sum = jnp.sum(expo, axis=-1)
    update = jnp.einsum(
        "fqk,fkc->fqc", expo.astype(jnp.bfloat16), values, preferred_element_type=jnp.float32
    )
    return (new_max, new_sum, update)


def body(frames, segment_ids, norm_gain, conv_weight, attn_gain, w_qkv, w_out):
    depth, height, across, width = frames.shape
    inputs = frames.astype(jnp.float32)
    activated = jax.nn.silu(normalize(inputs, norm_gain)).astype(jnp.bfloat16)
    first = lax.axis_index("tm") * depth
    padded_ids = jnp.concatenate([jnp.full((2,), -1, jnp.int32), segment_ids])
    local_ids = lax.dynamic_slice_in_dim(padded_ids, first, depth + 2)
    own_ids = local_ids[2:]
    earlier = passed_along(activated, "tm", 1)
    extended = with_halo(jnp.concatenate([earlier, activated], 0), (("rows", 1),), 1)
    extended = jnp.pad(extended, ((0, 0), (0, 0), (1, 1), (0, 0)))
    masked = jnp.stack(
        [
            extended[tap_t : tap_t + depth]
            * (local_ids[tap_t : tap_t + depth] == own_ids).astype(jnp.bfloat16)[
                :, None, None, None
            ]
            for tap_t in range(3)
        ]
    )
    total = jnp.zeros((depth, height, across, width), jnp.float32)
    piece = lax.all_gather(conv_weight, "tm", axis=0, tiled=True)
    for tap_t in range(3):
        for tap_h in range(3):
            for tap_w in range(3):
                window = masked[tap_t, :, tap_h : tap_h + height, tap_w : tap_w + across, :]
                total = total + jnp.einsum(
                    "fhwc,cd->fhwd",
                    window,
                    piece[:, tap_t, tap_h, tap_w, :],
                    preferred_element_type=jnp.float32,
                )
    summed = (inputs + total).astype(jnp.bfloat16)
    normed = normalize(summed.astype(jnp.float32), attn_gain).astype(jnp.bfloat16)
    flat = normed.reshape(depth, height * across, width)
    positions = height * across
    initial = (
        jnp.full((depth, positions), -1e30, jnp.float32),
        jnp.zeros((depth, positions), jnp.float32),
        jnp.zeros((depth, positions, width), jnp.float32),
    )
    projected = jnp.einsum("fpc,cd->fpd", flat, w_qkv, preferred_element_type=jnp.float32)
    queries = projected[:, :, :width].astype(jnp.bfloat16)
    keys = projected[:, :, width : 2 * width].astype(jnp.bfloat16)
    values = projected[:, :, 2 * width :].astype(jnp.bfloat16)
    result = absorb(
        initial,
        queries,
        lax.all_gather(keys, "rows", axis=1, tiled=True),
        lax.all_gather(values, "rows", axis=1, tiled=True),
    )
    mixed = (result[2] / result[1][:, :, None]).astype(jnp.bfloat16)
    attended = jnp.einsum("fpc,cd->fpd", mixed, w_out, preferred_element_type=jnp.float32).astype(
        jnp.bfloat16
    )
    return (summed, attended.reshape(depth, height, across, width))


def solution(mesh):
    return jax.shard_map(
        body,
        mesh=mesh,
        in_specs=(
            P(("groups", "tm"), "rows", None, None),
            P("groups"),
            P(),
            P("tm", None, None, None, None),
            P(),
            P(),
            P(),
        ),
        out_specs=(
            P(("groups", "tm"), "rows", None, None),
            P(("groups", "tm"), "rows", None, None),
        ),
        check_vma=False,
    )
```

profile of v0, /device:TPU:0, one launch (start us, length us, event | category | flops | bytes accessed | tf_op | source)
XLA Modules:
  0.0 109.3 jit_solution(11595959502786143443)
XLA Ops:
  7.2 0.0 copy-start
  7.2 0.0 all-gather.2.cloned.1.call-start
  7.2 0.7 all-gather.2.cloned.1.call-update
  7.9 1.1 %fusion.15 = f32[2,160]{1,0:T(2,128)S(1)} fusion(bf16[2,1,160,384]{3,2,1,0:T(8,128)(2,1)} %param.7), kind=kLoop, calls=%fused_computation.56 | loop fusion | flops 368320 | bytes 247040 | tf_op jit(solution)/shard_map/reduce_sum | solution.py:36
  9.0 1.2 %fusion.22 = bf16[2,1,160,384]{3,2,0,1:T(8,128)(2,1)S(1)} fusion(bf16[2,1,160,384]{3,2,1,0:T(8,128)(2,1)} %param.7, f32[384]{0:T(512)} %param.9, f32[2,160]{1,0:T(2,128)S(1)} %add_rsqrt_fusion.1), kind=kLoop, calls=%fused_computation.63 | loop fusion | flops 983040 | bytes 494336 | tf_op jit(solution)/shard_map/convert_element_type | solution.py:57
  10.2 2.4 %collective-permute-start = (bf16[2,1,160,384]{3,2,0,1:T(8,128)(2,1)S(1)}, bf16[2,1,160,384]{3,2,0,1:T(8,128)(2,1)S(1)}, u32[]{:S(2)}, u32[]{:S(2)}) collective-permute-start(bf16[2,1,160,384]{3,2,0,1:T(8,128)(2,1)S(1)} %fusion.22), channel_id=1, source_target_pairs={{0,1},{1,2},{2,3},{3,4},{4,5},{5,6},{6,7},{7,8},{8,9},{9,10},{10,1... | collective-permute-start | bytes 737288 | tf_op jit(solution)/shard_map/ppermute | solution.py:15
  12.6 1.1 %collective-permute-done = bf16[2,1,160,384]{3,2,0,1:T(8,128)(2,1)S(1)} collective-permute-done((bf16[2,1,160,384]{3,2,0,1:T(8,128)(2,1)S(1)}, bf16[2,1,160,384]{3,2,0,1:T(8,128)(2,1)S(1)}, u32[]{:S(2)}, u32[]{:S(2)}) %collective-permute-start) | collective-permute-done | bytes 245792 | tf_op jit(solution)/shard_map/ppermute | solution.py:15
  13.7 0.1 pad_maximum_fusion
  13.8 0.7 collective-permute-start.1
  14.5 0.7 pad_dynamic-slice_fusion
  15.2 0.1 compare_convert_fusion
  15.3 0.3 select_maximum_fusion
  15.6 0.3 slice_bitcast_fusion
  15.9 68.5 %all-gather.2.cloned.1.call-done = bf16[384,3,3,3,384]{4,0,3,2,1:T(8,128)(2,1)} async-done(((bf16[24,3,3,3,384]{4,0,3,2,1:T(8,128)(2,1)}), bf16[384,3,3,3,384]{4,0,3,2,1:T(8,128)(2,1)}) %all-gather.2.cloned.1.call-update) | async-done | bytes 7962640 | tf_op jit(solution)/shard_map/all_gather | solution.py:75
  84.4 1.4 %fusion.23 = f32[2,160,384]{2,1,0:T(8,128)S(1)} fusion(bf16[384,3,3,3,384]{4,0,3,2,1:T(8,128)(2,1)} %all-gather.2.cloned.1.call-done, bf16[1,2,3,162,384]{4,3,1,2,0:T(8,128)(2,1)S(1)} %get-tuple-element.6), kind=kOutput, calls=%fused_computation.93 | convolution fusion | flops 94371840 | bytes 1032192 | tf_op jit(solution)/shard_map/fhwc,cd->fhwd/dot_general | solution.py:80
  85.8 1.7 %convolution_add_fusion.25 = f32[2,160,384]{2,1,0:T(8,128)S(1)} fusion(f32[2,160,384]{2,1,0:T(8,128)S(1)} %fusion.23, bf16[384,3,3,3,384]{4,0,3,2,1:T(8,128)(2,1)} %all-gather.2.cloned.1.call-done, bf16[1,2,3,162,384]{4,3,1,2,0:T(8,128)(2,1)S(1)} %get-tuple-element.6), kind=kOutput, calls=%fused_computation.36 | convolution fusion | flops 94494720 | bytes 1523712 | tf_op jit(solution)/shard_map/fhwc,cd->fhwd/dot_general | solution.py:80
  87.5 1.3 %convolution_add_fusion.24 = f32[2,160,384]{2,1,0:T(8,128)S(1)} fusion(f32[2,160,384]{2,1,0:T(8,128)S(1)} %convolution_add_fusion.25, bf16[384,3,3,3,384]{4,0,3,2,1:T(8,128)(2,1)} %all-gather.2.cloned.1.call-done, bf16[1,2,3,162,384]{4,3,1,2,0:T(8,128)(2,1)S(1)} %get-tuple-element.6), kind=kOutput, calls=%fused_computation.35 | convolution fusion | flops 94494720 | bytes 1523712 | tf_op jit(solution)/shard_map/fhwc,cd->fhwd/dot_general | solution.py:80
  88.8 1.3 %convolution_add_fusion.23 = f32[2,160,384]{2,1,0:T(8,128)S(1)} fusion(f32[2,160,384]{2,1,0:T(8,128)S(1)} %convolution_add_fusion.24, bf16[384,3,3,3,384]{4,0,3,2,1:T(8,128)(2,1)} %all-gather.2.cloned.1.call-done, bf16[1,2,3,162,384]{4,3,1,2,0:T(8,128)(2,1)S(1)} %get-tuple-element.6), kind=kOutput, calls=%fused_computation.34 | convolution fusion | flops 94494720 | bytes 1523712 | tf_op jit(solution)/shard_map/fhwc,cd->fhwd/dot_general | solution.py:80
  90.1 1.3 %convolution_add_fusion.22 = f32[2,160,384]{2,1,0:T(8,128)S(1)} fusion(f32[2,160,384]{2,1,0:T(8,128)S(1)} %convolution_add_fusion.23, bf16[384,3,3,3,384]{4,0,3,2,1:T(8,128)(2,1)} %all-gather.2.cloned.1.call-done, bf16[1,2,3,162,384]{4,3,1,2,0:T(8,128)(2,1)S(1)} %get-tuple-element.6), kind=kOutput, calls=%fused_computation.33 | convolution fusion | flops 94494720 | bytes 1523712 | tf_op jit(solution)/shard_map/fhwc,cd->fhwd/dot_general | solution.py:80
  91.4 1.3 %convolution_add_fusion.21 = f32[2,160,384]{2,1,0:T(8,128)S(1)} fusion(f32[2,160,384]{2,1,0:T(8,128)S(1)} %convolution_add_fusion.22, bf16[384,3,3,3,384]{4,0,3,2,1:T(8,128)(2,1)} %all-gather.2.cloned.1.call-done, bf16[1,2,3,162,384]{4,3,1,2,0:T(8,128)(2,1)S(1)} %get-tuple-element.6), kind=kOutput, calls=%fused_computation.32 | convolution fusion | flops 94494720 | bytes 1523712 | tf_op jit(solution)/shard_map/fhwc,cd->fhwd/dot_general | solution.py:80
  92.7 0.3 convolution_add_fusion.20
  93.1 0.3 convolution_add_fusion.19
  93.4 0.3 convolution_add_fusion.18
  93.8 0.3 convolution_add_fusion.17
  94.1 0.3 convolution_add_fusion.16
  94.5 0.3 convolution_add_fusion.15
  94.8 0.3 convolution_add_fusion.14
  95.2 0.3 convolution_add_fusion.13
  95.5 0.3 convolution_add_fusion.12
  95.8 0.3 convolution_add_fusion.11
  96.2 0.0 copy-start.2
  96.2 0.3 convolution_add_fusion.10
  96.5 0.0 copy-start.4
  96.6 0.3 convolution_add_fusion.9
  96.9 0.3 convolution_add_fusion.8
  97.3 0.3 convolution_add_fusion.7
  97.6 0.3 convolution_add_fusion.6
  98.0 0.3 convolution_add_fusion.5
  98.3 0.3 convolution_add_fusion.4
  98.6 0.3 convolution_add_fusion.3
  99.0 0.3 convolution_add_fusion.2
  99.3 0.3 convolution_add_fusion.1
  99.7 0.5 fusion.12
  100.2 0.0 copy-start.3
  100.2 0.6 convolution_convert_fusion
  100.8 0.3 fusion.40
  101.1 0.1 fusion.25
  101.2 1.2 %fusion.8 = bf16[2,1,160,384]{3,2,1,0:T(8,128)(2,1)} fusion(bf16[384,384]{1,0:T(8,128)(2,1)S(1)} %copy-done.5, bf16[2,160,1152]{2,1,0:T(8,128)(2,1)S(1)} %convolution_convert_fusion, f32[2,160]{1,0:T(2,128)S(1)} %fusion.25, f32[2,160,160]{1,2,0:T(8,128)S(1)} %get-tuple-element.12, f32[2,160]{1,0:T(2,128)S(1)} %broadcast_maximum_fusion), kind=kOutput, calls=%fused_computation.42 | convolution fusion | flops 134164480 | bytes 1118208 | tf_op jit(solution)/shard_map/fpc,cd->fpd/dot_general | solution.py:106
  (12 shorter events, 0.0 us)
Async XLA Ops:
  7.2 93.0 %copy-start = (bf16[384,1152]{1,0:T(8,128)(2,1)S(1)}, bf16[384,1152]{1,0:T(8,128)(2,1)}, u32[]{:S(2)}) copy-start(bf16[384,1152]{1,0:T(8,128)(2,1)} %param.12) | copy-start | bytes 2654212
  7.2 77.2 %all-gather.2.cloned.1.call-start = ((), (), s32[]{:S(2)}) async-start(), calls=%async_computation | async-start | bytes 8460288 | tf_op jit(solution)/shard_map/all_gather | solution.py:75
  10.2 3.5 %collective-permute-start = (bf16[2,1,160,384]{3,2,0,1:T(8,128)(2,1)S(1)}, bf16[2,1,160,384]{3,2,0,1:T(8,128)(2,1)S(1)}, u32[]{:S(2)}, u32[]{:S(2)}) collective-permute-start(bf16[2,1,160,384]{3,2,0,1:T(8,128)(2,1)S(1)} %fusion.22), channel_id=1, source_target_pairs={{0,1},{1,2},{2,3},{3,4},{4,5},{5,6},{6,7},{7,8},{8,9},{9,10},{10,1... | collective-permute-start | bytes 737288 | tf_op jit(solution)/shard_map/ppermute | solution.py:15
  13.8 1.5 %collective-permute-start.1 = (bf16[4,1,160,384]{3,2,0,1:T(8,128)(2,1)S(1)}, bf16[4,1,160,384]{3,2,0,1:T(8,128)(2,1)S(1)}, u32[]{:S(2)}, u32[]{:S(2)}) collective-permute-start(bf16[4,1,160,384]{3,2,0,1:T(8,128)(2,1)S(1)} %pad_maximum_fusion), channel_id=1, source_target_pairs={} | collective-permute-start | bytes 1474568 | tf_op jit(solution)/shard_map/ppermute | solution.py:26
  84.4 8.4 %copy-start.1 = (bf16[384,3,3,3,384]{4,0,3,2,1:T(8,128)(2,1)S(1)}, bf16[384,3,3,3,384]{4,0,3,2,1:T(8,128)(2,1)}, u32[]{:S(2)}) copy-start(bf16[384,3,3,3,384]{4,0,3,2,1:T(8,128)(2,1)} %all-gather.2.cloned.1.call-done) | copy-start | bytes 23887876
  96.2 3.5 %copy-start.2 = (bf16[2,1,160,384]{3,2,1,0:T(8,128)(2,1)S(1)}, bf16[2,1,160,384]{3,2,1,0:T(8,128)(2,1)}, u32[]{:S(2)}) copy-start(bf16[2,1,160,384]{3,2,1,0:T(8,128)(2,1)} %param.7) | copy-start | bytes 737284
  96.5 3.7 %copy-start.4 = (f32[384]{0:T(512)S(1)}, f32[384]{0:T(512)}, u32[]{:S(2)}) copy-start(f32[384]{0:T(512)} %param.11) | copy-start | bytes 4612
  97.2 4.0 %copy-start.5 = (bf16[384,384]{1,0:T(8,128)(2,1)S(1)}, bf16[384,384]{1,0:T(8,128)(2,1)}, u32[]{:S(2)}) copy-start(bf16[384,384]{1,0:T(8,128)(2,1)} %param.13) | copy-start | bytes 884740
  100.2 2.2 %copy-start.3 = (bf16[2,1,160,384]{3,2,0,1:T(8,128)(2,1)}, bf16[2,1,160,384]{3,2,0,1:T(8,128)(2,1)S(1)}, u32[]{:S(2)}) copy-start(bf16[2,1,160,384]{3,2,0,1:T(8,128)(2,1)S(1)} %get-tuple-element.10) | copy-start | bytes 737284
Sparse Core Ops, SparseCore 0:
  10.2 74.1 all-gather.1
where the time goes:
time: 110 us; the launch traced here: 109 us
  waiting for transfers between devices  70.3 us (64%)
  matrix products  17.7 us (16%)
  between operations  14.4 us (13%)
  starting transfers between devices  3.13 us (3%)
  other arithmetic  3.03 us (3%)
    all_gather x1, waiting for transfers between devices, body(): piece = lax.all_gather(conv_weight, 'tm', axis=0, tiled=True)  68.5 us
    dot_general x27, matrix products, body(): jnp.einsum('fhwc,cd->fhwd', window, piece[:, tap_t, tap_h, tap_w, :], pre...  15.6 us
    ppermute x1, starting transfers between devices, passed_along(): lax.ppermute(value, axis, [(source, source + steps) for source in range(l...  2.41 us
  transfers between devices with their start and end apart: 3, of which 2 were waited for; matrix products, arithmetic and copies ran while one was open for 3% of the time, Pallas kernels for 0%

commit v1 on v0

--- a/solution.py
+++ b/solution.py
@@ -1,6 +1,7 @@
 import jax
 import jax.numpy as jnp
 from jax import lax
+from jax.sharding import Mesh
 from jax.sharding import PartitionSpec as P
 
 C = 384
@@ -53,13 +54,18 @@
 
 def body(frames, segment_ids, norm_gain, conv_weight, attn_gain, w_qkv, w_out):
     depth, height, across, width = frames.shape
+    chips = lax.axis_size("chip")
+    core = lax.axis_index("core")
     inputs = frames.astype(jnp.float32)
     activated = jax.nn.silu(normalize(inputs, norm_gain)).astype(jnp.bfloat16)
-    first = lax.axis_index("tm") * depth
+    position = lax.axis_index("chip") * 2 + core
+    first = position * depth
     padded_ids = jnp.concatenate([jnp.full((2,), -1, jnp.int32), segment_ids])
     local_ids = lax.dynamic_slice_in_dim(padded_ids, first, depth + 2)
     own_ids = local_ids[2:]
-    earlier = passed_along(activated, "tm", 1)
+    earlier = lax.ppermute(
+        activated, ("chip", "core"), [(source, source + 1) for source in range(2 * chips - 1)]
+    )
     extended = with_halo(jnp.concatenate([earlier, activated], 0), (("rows", 1),), 1)
     extended = jnp.pad(extended, ((0, 0), (0, 0), (1, 1), (0, 0)))
     masked = jnp.stack(
@@ -71,18 +77,29 @@
             for tap_t in range(3)
         ]
     )
-    total = jnp.zeros((depth, height, across, width), jnp.float32)
-    piece = lax.all_gather(conv_weight, "tm", axis=0, tiled=True)
+    share = width // (2 * chips)
+    sets = masked.reshape(masked.shape[:-1] + (chips, 2, share))
+    first_set = sets[..., 0, :].reshape(masked.shape[:-1] + (chips * share,))
+    second_set = sets[..., 1, :].reshape(masked.shape[:-1] + (chips * share,))
+    mine = jnp.where(core == 0, first_set, second_set)
+    other = jnp.where(core == 0, second_set, first_set)
+    swap = [(0, 1), (1, 0)]
+    received = lax.ppermute(other, "core", swap)
+    both = jnp.concatenate([mine, received], axis=1)
+    total = jnp.zeros((2 * depth, height, across, width), jnp.float32)
+    piece = lax.all_gather(conv_weight, "chip", axis=0, tiled=True)
     for tap_t in range(3):
         for tap_h in range(3):
             for tap_w in range(3):
-                window = masked[tap_t, :, tap_h : tap_h + height, tap_w : tap_w + across, :]
+                window = both[tap_t, :, tap_h : tap_h + height, tap_w : tap_w + across, :]
                 total = total + jnp.einsum(
                     "fhwc,cd->fhwd",
                     window,
                     piece[:, tap_t, tap_h, tap_w, :],
                     preferred_element_type=jnp.float32,
                 )
+    returned = lax.ppermute(total[depth:], "core", swap)
+    total = total[:depth] + returned
     summed = (inputs + total).astype(jnp.bfloat16)
     normed = normalize(summed.astype(jnp.float32), attn_gain).astype(jnp.bfloat16)
     flat = normed.reshape(depth, height * across, width)
@@ -110,21 +127,23 @@
 
 
 def solution(mesh):
+    groups, tm, rows = mesh.devices.shape
+    split = Mesh(mesh.devices.reshape(groups, tm // 2, 2, rows), ("groups", "chip", "core", "rows"))
     return jax.shard_map(
         body,
-        mesh=mesh,
+        mesh=split,
         in_specs=(
-            P(("groups", "tm"), "rows", None, None),
+            P(("groups", "chip", "core"), "rows", None, None),
             P("groups"),
             P(),
-            P("tm", None, None, None, None),
+            P(("chip", "core"), None, None, None, None),
             P(),
             P(),
             P(),
         ),
         out_specs=(
-            P(("groups", "tm"), "rows", None, None),
-            P(("groups", "tm"), "rows", None, None),
+            P(("groups", "chip", "core"), "rows", None, None),
+            P(("groups", "chip", "core"), "rows", None, None),
         ),
         check_vma=False,
     )

time: 110 us -> 135 us (1.23)
  other arithmetic: 3.03 us -> 39.2 us
  waiting for transfers between devices: 70.3 us -> 42.3 us
  local copies, waits for them, and re-layouts: 0.78 us -> 17.5 us
  starting transfers between devices: 3.13 us -> 7.79 us
  matrix products: 17.7 us -> 13.1 us
    all_gather x1, waiting for transfers between devices: 68.5 us -> 38.3 us  [body(): piece = lax.all_gather(conv_weight, 'chip', axis=0, tiled=True)]
    add x0 -> x2, other arithmetic: none -> 26.3 us  [body(): total + jnp.einsum('fhwc,cd->fhwd', window, piece[:, tap_t, tap_h, tap_w,...]
    select_n x0 -> x2, local copies, waits for them, and re-layouts: none -> 6.17 us  [the longest x1 3.31 us: body(): other = jnp.where(core == 0, second_set, first_set)]
    ppermute x1 -> x3, starting transfers between devices: 2.41 us -> 7.06 us  [the longest x1 4.58 us: body(): received = lax.ppermute(other, 'core', swap)]
    dot_general x27, matrix products: 15.6 us -> 11.1 us  [body(): jnp.einsum('fhwc,cd->fhwd', window, piece[:, tap_t, tap_h, tap_w, :], pre...]
    slice x0 -> x2, local copies, waits for them, and re-layouts: none -> 3.55 us  [the longest x1 3.29 us: body(): extended[tap_t:tap_t + depth]]
    mul x0 -> x1, other arithmetic: none -> 3.41 us  [body(): extended[tap_t:tap_t + depth]]
    mul x0 -> x2, local copies, waits for them, and re-layouts: none -> 3.22 us  [body(): extended[tap_t:tap_t + depth]]
  transfers between devices with their start and end apart: 3 -> 5, of which waited for: 2 -> 4; matrix products, arithmetic and copies ran while one was open for 3% -> 21% of each run, Pallas kernels for 0% -> 0%
where the time goes in v1:
time: 135 us; the launch traced here: 134 us
  waiting for transfers between devices  42.3 us (31%)
  other arithmetic  39.2 us (29%)
  local copies, waits for them, and re-layouts  17.5 us (13%)
  between operations  14.4 us (11%)
  matrix products  13.1 us (10%)
  starting transfers between devices  7.79 us (6%)
    all_gather x1, waiting for transfers between devices, body(): piece = lax.all_gather(conv_weight, 'chip', axis=0, tiled=True)  38.3 us
    add x2, other arithmetic, body(): total + jnp.einsum('fhwc,cd->fhwd', window, piece[:, tap_t, tap_h, tap_w,...  26.3 us
    dot_general x27, matrix products, body(): jnp.einsum('fhwc,cd->fhwd', window, piece[:, tap_t, tap_h, tap_w, :], pre...  11.1 us
    ppermute x1, starting transfers between devices, body(): received = lax.ppermute(other, 'core', swap)  4.58 us
    mul x1, other arithmetic, body(): extended[tap_t:tap_t + depth]  3.41 us
    select_n x1, local copies, waits for them, and re-layouts, body(): other = jnp.where(core == 0, second_set, first_set)  3.31 us
    slice x1, local copies, waits for them, and re-layouts, body(): extended[tap_t:tap_t + depth]  3.29 us
    mul x2, local copies, waits for them, and re-layouts, body(): extended[tap_t:tap_t + depth]  3.22 us
  transfers between devices with their start and end apart: 5, of which 4 were waited for; matrix products, arithmetic and copies ran while one was open for 21% of the time, Pallas kernels for 0%

profile of v1, /device:TPU:0, one launch (start us, length us, event | category | flops | bytes accessed | tf_op | source)
XLA Modules:
  0.0 134.3 jit_solution(2010087847825651294)
XLA Ops:
  7.2 0.7 all-gather.2.cloned.1.call-update
  7.9 1.3 fusion.10
  9.2 1.6 %fusion.14 = bf16[2,1,160,384]{3,0,2,1:T(2,128)(2,1)S(1)} fusion(f32[384]{0:T(512)} %param.9, f32[2,160]{0,1:T(8,128)S(1)} %add_rsqrt_fusion.1, bf16[2,1,160,384]{3,2,1,0:T(8,128)(2,1)} %param.7), kind=kLoop, calls=%fused_computation.114 | loop fusion | flops 983040 | bytes 494336 | tf_op jit(solution)/shard_map/convert_element_type | solution.py:60
  10.8 2.4 %collective-permute-start = (bf16[2,1,160,384]{3,0,2,1:T(2,128)(2,1)S(1)}, bf16[2,1,160,384]{3,0,2,1:T(2,128)(2,1)S(1)}, u32[]{:S(2)}, u32[]{:S(2)}) collective-permute-start(bf16[2,1,160,384]{3,0,2,1:T(2,128)(2,1)S(1)} %fusion.14), channel_id=1, source_target_pairs={{0,1},{1,2},{2,3},{3,4},{4,5},{5,6},{6,7},{7,8},{8,9},{9,10},{10,1... | collective-permute-start | bytes 737288 | tf_op jit(solution)/shard_map/ppermute | solution.py:66
  13.3 1.1 collective-permute-done
  14.4 0.5 pad_maximum_fusion.1
  14.9 0.7 collective-permute-start.1
  15.8 1.8 %select_maximum_fusion = bf16[4,3,162,384]{3,0,2,1:T(4,128)(2,1)S(1)} fusion(bf16[4,1,160,384]{3,0,2,1:T(4,128)(2,1)S(1)} %collective-permute-done.1, bf16[2,1,160,384]{3,0,2,1:T(2,128)(2,1)S(1)} %fusion.14, bf16[2,1,160,384]{3,0,2,1:T(2,128)(2,1)S(1)} %collective-permute-done), kind=kLoop, calls=%fused_computation.59 | loop fusion | flops 11197440 | bytes 2476032 | tf_op jit(solution)/shard_map/concatenate | solution.py:25
  17.5 3.4 %slice_multiply_fusion.1 = (bf16[2,3,162,384]{3,0,2,1:T(2,128)(2,1)S(1)}, bf16[2,3,162,384]{3,0,2,1:T(2,128)(2,1)}, bf16[2,3,162,384]{3,0,2,1:T(2,128)(2,1)}) fusion(bf16[4,3,162,384]{3,0,2,1:T(4,128)(2,1)S(1)} %select_maximum_fusion, bf16[2]{0:T(256)(128)(2,1)S(1)} %get-tuple-element.17, bf16[2]{0:T(256)(128)(2,1)S(1)} %get-tuple-element.18), kind=kLoop, calls=%fused_computation.97 | loop fusion | flops 746496 | bytes 4478984 | tf_op jit(solution)/shard_map/mul | solution.py:73
  20.9 0.9 copy.34
  21.8 2.4 %copy.35 = bf16[2,3,162,384]{2,3,1,0:T(8,128)(2,1)S(1)} copy(bf16[2,3,162,384]{3,0,2,1:T(2,128)(2,1)} %get-tuple-element.15) | data formatting | bytes 1492992 | tf_op jit(solution)/shard_map/mul | solution.py:73
  24.2 3.3 %copy.36 = bf16[2,3,162,384]{2,3,1,0:T(8,128)(2,1)} copy(bf16[2,3,162,384]{3,0,2,1:T(2,128)(2,1)} %get-tuple-element.16) | data formatting | bytes 1492992 | tf_op jit(solution)/shard_map/slice | solution.py:73
  27.5 1.9 %pad_maximum_fusion = bf16[3,2,3,162,8,2,24]{3,6,5,4,2,1,0:T(8,128)(2,1)S(1)} fusion(bf16[1,2,3,162,8,2,24]{3,6,5,4,2,1,0:T(8,128)(2,1)} %bitcast.246, bf16[1,2,3,162,8,2,24]{3,6,5,4,2,1,0:T(8,128)(2,1)S(1)} %bitcast.245, bf16[1,2,3,162,8,2,24]{3,6,5,4,2,1,0:T(8,128)(2,1)S(1)} %bitcast.244), kind=kLoop, calls=%fused_computation.54 | loop fusion | flops 2239488 | bytes 4478976 | tf_op jit(solution)/shard_map/stack | solution.py:71
  29.4 1.5 %broadcast_select_fusion.1 = (bf16[3,2,3,162,8,1,24]{3,6,5,4,2,1,0:T(8,128)(2,1)}, bf16[3,2,3,162,8,1,24]{3,6,5,4,2,1,0:T(8,128)(2,1)S(1)}) fusion(pred[]{:T(512)S(6)} %eq.11, bf16[3,2,3,162,8,2,24]{3,6,5,4,2,1,0:T(8,128)(2,1)S(1)} %pad_maximum_fusion), kind=kLoop, calls=%fused_computation.58 | loop fusion | flops 1119744 | bytes 4478977 | tf_op jit(solution)/shard_map/jit(_where)/select_n | solution.py:84
  30.8 3.3 %copy.37 = bf16[3,2,3,162,192]{4,1,3,2,0:T(2,128)(2,1)} copy(bf16[3,2,3,162,192]{3,4,2,1,0:T(8,128)(2,1)S(1)} %bitcast.243) | data formatting | bytes 2239488 | tf_op jit(solution)/shard_map/jit(_where)/select_n | solution.py:85
  34.1 4.6 %collective-permute-start.2 = (bf16[3,2,3,162,192]{4,1,3,2,0:T(2,128)(2,1)}, bf16[3,2,3,162,192]{4,1,3,2,0:T(2,128)(2,1)}, u32[]{:S(2)}, u32[]{:S(2)}) collective-permute-start(bf16[3,2,3,162,192]{4,1,3,2,0:T(2,128)(2,1)} %copy.37), channel_id=1, source_target_pairs={{0,1},{1,0},{2,3},{3,2},{4,5},{5,4},{6,7},{7,6},{8,9},{9,8},{10,11... | collective-permute-start | bytes 3359240 | tf_op jit(solution)/shard_map/ppermute | solution.py:87
  38.7 2.9 %copy.38 = bf16[3,2,3,162,192]{4,3,1,2,0:T(8,128)(2,1)S(1)} copy(bf16[3,2,3,162,192]{3,4,2,1,0:T(8,128)(2,1)} %bitcast.242) | data formatting | bytes 2239488 | tf_op jit(solution)/shard_map/jit(_where)/select_n | solution.py:84
  41.6 0.4 collective-permute-done.2
  42.0 2.8 %copy.39 = bf16[3,2,3,162,192]{4,3,1,2,0:T(8,128)(2,1)} copy(bf16[3,2,3,162,192]{4,1,3,2,0:T(2,128)(2,1)} %collective-permute-done.2) | data formatting | bytes 2239488 | tf_op jit(solution)/shard_map/ppermute | solution.py:87
  44.7 38.3 %all-gather.2.cloned.1.call-done = bf16[192,3,3,3,384]{4,0,3,2,1:T(8,128)(2,1)} async-done(((bf16[24,3,3,3,384]{4,0,3,2,1:T(8,128)(2,1)}), bf16[192,3,3,3,384]{4,0,3,2,1:T(8,128)(2,1)}) %all-gather.2.cloned.1.call-update) | async-done | bytes 3981328 | tf_op jit(solution)/shard_map/all_gather | solution.py:90
  83.0 1.4 %fusion.95 = f32[4,160,384]{2,1,0:T(8,128)S(1)} fusion(bf16[3,2,3,162,192]{4,3,1,2,0:T(8,128)(2,1)S(1)} %copy.38, bf16[3,2,3,162,192]{4,3,1,2,0:T(8,128)(2,1)} %copy.39, bf16[192,3,3,3,384]{4,0,3,2,1:T(8,128)(2,1)} %all-gather.2.cloned.1.call-done), kind=kOutput, calls=%fused_computation.195 | convolution fusion | flops 94494720 | bytes 3798528 | tf_op jit(solution)/shard_map/fhwc,cd->fhwd/dot_general | solution.py:95
  84.6 1.4 %fusion.93 = f32[4,160,384]{2,1,0:T(8,128)S(1)} fusion(bf16[3,2,3,162,192]{4,3,1,2,0:T(8,128)(2,1)S(1)} %copy.38, bf16[3,2,3,162,192]{4,3,1,2,0:T(8,128)(2,1)S(1)} %copy-done.1, bf16[192,3,3,3,384]{4,0,3,2,1:T(8,128)(2,1)} %all-gather.2.cloned.1.call-done), kind=kOutput, calls=%fused_computation.193 | convolution fusion | flops 94494720 | bytes 3369984 | tf_op jit(solution)/shard_map/fhwc,cd->fhwd/dot_general | solution.py:95
  86.0 0.8 copy-done.2
  86.8 0.3 fusion.91
  87.1 1.6 %copy_add_fusion.24 = f32[4,160,384]{2,0,1:T(4,128)S(1)} fusion(f32[4,160,384]{2,1,0:T(8,128)S(1)} %fusion.91, f32[4,160,384]{2,1,0:T(8,128)S(1)} %fusion.93, f32[4,160,384]{2,1,0:T(8,128)S(1)} %fusion.95), kind=kLoop, calls=%fused_computation.93 | loop fusion | flops 491520 | bytes 3932160 | tf_op jit(solution)/shard_map/add | solution.py:95
  89.1 0.3 fusion.87
  89.4 0.3 fusion.85
  89.8 0.3 fusion.83
  90.5 0.3 fusion.79
  91.5 0.3 fusion.73
  91.8 0.3 fusion.71
  92.1 0.3 fusion.69
  92.5 0.3 fusion.67
  92.8 0.3 fusion.65
  93.5 0.3 fusion.61
  94.5 0.3 fusion.55
  94.8 0.3 fusion.53
  95.1 0.3 fusion.51
  95.5 0.3 fusion.49
  95.8 0.3 fusion.47
  96.2 0.3 fusion.42
  96.5 0.3 fusion.45
  96.8 24.7 %copy_add_fusion = f32[4,160,384]{2,0,1:T(4,128)S(1)} fusion(f32[4,160,384]{2,1,0:T(8,128)S(1)} %fusion.42, f32[4,160,384]{2,1,0:T(8,128)S(1)} %fusion.45, f32[4,160,384]{2,1,0:T(8,128)S(1)} %fusion.47, f32[4,160,384]{2,1,0:T(8,128)S(1)} %fusion.49, f32[4,160,384]{2,1,0:T(8,128)S(1)} %fusion.51, f32[4,160,384]{2,1,0:T(8,128)S(1)} %fusion.53, ...), kind=kLoop, calls=%fused_computation.69 | loop fusion | flops 5898240 | bytes 25559040 | tf_op jit(solution)/shard_map/add | solution.py:95
  121.8 1.9 %collective-permute-done.3 = f32[2,1,160,384]{3,0,2,1:T(2,128)S(1)} collective-permute-done((f32[2,1,160,384]{3,0,2,1:T(2,128)S(1)}, f32[2,1,160,384]{3,0,2,1:T(2,128)S(1)}, u32[]{:S(2)}, u32[]{:S(2)}) %collective-permute-start.3) | collective-permute-done | bytes 491552 | tf_op jit(solution)/shard_map/ppermute | solution.py:101
  123.7 0.5 fusion.7
  124.2 0.7 copy.69
  125.3 0.6 convolution_convert_fusion
  126.2 1.2 fusion.5
  (32 shorter events, 3.7 us)
Async XLA Ops:
  7.2 118.1 %copy-start = (bf16[384,1152]{1,0:T(8,128)(2,1)S(1)}, bf16[384,1152]{1,0:T(8,128)(2,1)}, u32[]{:S(2)}) copy-start(bf16[384,1152]{1,0:T(8,128)(2,1)} %param.12) | copy-start | bytes 2654212
  7.2 8.4 %copy-start.6 = (s32[32]{0:T(128)S(1)}, s32[32]{0:T(128)}, u32[]{:S(2)}) copy-start(s32[32]{0:T(128)} %param.8) | copy-start | bytes 388
  7.2 75.9 %all-gather.2.cloned.1.call-start = ((), (), s32[]{:S(2)}) async-start(), calls=%async_computation | async-start | bytes 4478976 | tf_op jit(solution)/shard_map/all_gather | solution.py:90
  10.8 3.5 %collective-permute-start = (bf16[2,1,160,384]{3,0,2,1:T(2,128)(2,1)S(1)}, bf16[2,1,160,384]{3,0,2,1:T(2,128)(2,1)S(1)}, u32[]{:S(2)}, u32[]{:S(2)}) collective-permute-start(bf16[2,1,160,384]{3,0,2,1:T(2,128)(2,1)S(1)} %fusion.14), channel_id=1, source_target_pairs={{0,1},{1,2},{2,3},{3,4},{4,5},{5,6},{6,7},{7,8},{8,9},{9,10},{10,1... | collective-permute-start | bytes 737288 | tf_op jit(solution)/shard_map/ppermute | solution.py:66
  14.9 0.9 collective-permute-start.1
  34.1 7.8 %collective-permute-start.2 = (bf16[3,2,3,162,192]{4,1,3,2,0:T(2,128)(2,1)}, bf16[3,2,3,162,192]{4,1,3,2,0:T(2,128)(2,1)}, u32[]{:S(2)}, u32[]{:S(2)}) collective-permute-start(bf16[3,2,3,162,192]{4,1,3,2,0:T(2,128)(2,1)} %copy.37), channel_id=1, source_target_pairs={{0,1},{1,0},{2,3},{3,2},{4,5},{5,4},{6,7},{7,6},{8,9},{9,8},{10,11... | collective-permute-start | bytes 3359240 | tf_op jit(solution)/shard_map/ppermute | solution.py:87
  83.0 1.5 %copy-start.1 = (bf16[3,2,3,162,192]{4,3,1,2,0:T(8,128)(2,1)S(1)}, bf16[3,2,3,162,192]{4,3,1,2,0:T(8,128)(2,1)}, u32[]{:S(2)}) copy-start(bf16[3,2,3,162,192]{4,3,1,2,0:T(8,128)(2,1)} %copy.39) | copy-start | bytes 3359236
  84.6 2.2 %copy-start.2 = (bf16[192,3,3,3,384]{4,0,3,2,1:T(8,128)(2,1)S(1)}, bf16[192,3,3,3,384]{4,0,3,2,1:T(8,128)(2,1)}, u32[]{:S(2)}) copy-start(bf16[192,3,3,3,384]{4,0,3,2,1:T(8,128)(2,1)} %all-gather.2.cloned.1.call-done) | copy-start | bytes 11943940
  96.8 26.9 %copy-start.3 = (bf16[2,1,160,384]{3,2,1,0:T(8,128)(2,1)S(1)}, bf16[2,1,160,384]{3,2,1,0:T(8,128)(2,1)}, u32[]{:S(2)}) copy-start(bf16[2,1,160,384]{3,2,1,0:T(8,128)(2,1)} %param.7) | copy-start | bytes 737284
  121.5 3.5 %copy-start.4 = (f32[384]{0:T(512)S(1)}, f32[384]{0:T(512)}, u32[]{:S(2)}) copy-start(f32[384]{0:T(512)} %param.11) | copy-start | bytes 4612
  121.8 1.9 %collective-permute-start.3 = (f32[2,1,160,384]{3,0,2,1:T(2,128)S(1)}, f32[2,1,160,384]{3,0,2,1:T(2,128)S(1)}, u32[]{:S(2)}, u32[]{:S(2)}) collective-permute-start(f32[2,1,160,384]{3,0,2,1:T(2,128)S(1)} %slice_bitcast_fusion), channel_id=1, source_target_pairs={{0,1},{1,0},{2,3},{3,2},{4,5},{5,4},{6,7},{7,6},{8,9},{9,8},{10,11... | collective-permute-start | bytes 1474568 | tf_op jit(solution)/shard_map/ppermute | solution.py:101
  124.9 1.3 copy-start.5
Sparse Core Ops, SparseCore 0:
  10.3 72.7 all-gather.1

commit v2 on v1

--- a/solution.py
+++ b/solution.py
@@ -77,17 +77,13 @@
             for tap_t in range(3)
         ]
     )
-    share = width // (2 * chips)
-    sets = masked.reshape(masked.shape[:-1] + (chips, 2, share))
-    first_set = sets[..., 0, :].reshape(masked.shape[:-1] + (chips * share,))
-    second_set = sets[..., 1, :].reshape(masked.shape[:-1] + (chips * share,))
-    mine = jnp.where(core == 0, first_set, second_set)
-    other = jnp.where(core == 0, second_set, first_set)
     swap = [(0, 1), (1, 0)]
-    received = lax.ppermute(other, "core", swap)
-    both = jnp.concatenate([mine, received], axis=1)
+    received = lax.ppermute(masked, "core", swap)
+    both = jnp.concatenate([masked, received], axis=1)
     total = jnp.zeros((2 * depth, height, across, width), jnp.float32)
-    piece = lax.all_gather(conv_weight, "chip", axis=0, tiled=True)
+    gathered = lax.all_gather(conv_weight, "chip", axis=0)
+    keep = (lax.broadcasted_iota(jnp.int32, (1, 2, 1, 1, 1, 1, 1), 1) == core).astype(jnp.bfloat16)
+    piece = (gathered[:, None] * keep).reshape((width,) + conv_weight.shape[1:])
     for tap_t in range(3):
         for tap_h in range(3):
             for tap_w in range(3):

time: 135 us -> 118 us (0.87)
  other arithmetic: 39.2 us -> 13 us
  waiting for transfers between devices: 42.3 us -> 57.9 us
  local copies, waits for them, and re-layouts: 17.5 us -> 6.02 us
  matrix products: 13.1 us -> 18.7 us
    add x2 -> x0, other arithmetic: 26.3 us -> none  [body(): total + jnp.einsum('fhwc,cd->fhwd', window, piece[:, tap_t, tap_h, tap_w,...]
    all_gather x1, waiting for transfers between devices: 38.3 us -> 50.1 us  [body(): gathered = lax.all_gather(conv_weight, 'chip', axis=0)]
    select_n x2 -> x0, local copies, waits for them, and re-layouts: 6.17 us -> none  [the longest x1 3.31 us: body(): other = jnp.where(core == 0, second_set, first_set)]
    dot_general x27, matrix products: 11.1 us -> 16.6 us  [body(): jnp.einsum('fhwc,cd->fhwd', window, piece[:, tap_t, tap_h, tap_w, :], pre...]
    ppermute x1, waiting for transfers between devices: 0.39 us -> 4.15 us  [body(): received = lax.ppermute(masked, 'core', swap)]
    slice x1 -> x0, local copies, waits for them, and re-layouts: 3.29 us -> none  [body(): extended[tap_t:tap_t + depth]]
    mul x1, other arithmetic: 3.41 us -> 6.67 us  [body(): piece = (gathered[:, None] * keep).reshape((width,) + conv_weight.shape[1:])]
    another operation x0 -> x1, local copies, waits for them, and re-layouts: none -> 3.09 us  [body(): jnp.stack([extended[tap_t:tap_t + depth] * (local_ids[tap_t:tap_t + depth...]
  transfers between devices with their start and end apart: 5 -> 5, of which waited for: 4 -> 4; matrix products, arithmetic and copies ran while one was open for 21% -> 10% of each run, Pallas kernels for 0% -> 0%
where the time goes in v2:
time: 118 us
  waiting for transfers between devices  57.9 us (49%)
  matrix products  18.7 us (16%)
  between operations  14.4 us (12%)
  other arithmetic  13 us (11%)
  starting transfers between devices  7.8 us (7%)
  local copies, waits for them, and re-layouts  6.02 us (5%)
    all_gather x1, waiting for transfers between devices, body(): gathered = lax.all_gather(conv_weight, 'chip', axis=0)  50.1 us
    dot_general x27, matrix products, body(): jnp.einsum('fhwc,cd->fhwd', window, piece[:, tap_t, tap_h, tap_w, :], pre...  16.6 us
    mul x1, other arithmetic, body(): piece = (gathered[:, None] * keep).reshape((width,) + conv_weight.shape[1:])  6.67 us
    ppermute x1, starting transfers between devices, body(): received = lax.ppermute(masked, 'core', swap)  4.59 us
    ppermute x1, waiting for transfers between devices, body(): received = lax.ppermute(masked, 'core', swap)  4.15 us
    another operation x1, local copies, waits for them, and re-layouts, body(): jnp.stack([extended[tap_t:tap_t + depth] * (local_ids[tap_t:tap_t + depth...  3.09 us
    concatenate x1, other arithmetic, body(): both = jnp.concatenate([masked, received], axis=1)  2.8 us
    ppermute x1, starting transfers between devices, body(): lax.ppermute(activated, ('chip', 'core'), [(source, source + 1) for sourc...  2.41 us
  transfers between devices with their start and end apart: 5, of which 4 were waited for; matrix products, arithmetic and copies ran while one was open for 10% of the time, Pallas kernels for 0%

profile of v2, /device:TPU:0, one launch (start us, length us, event | category | flops | bytes accessed | tf_op | source)
XLA Modules:
  0.0 117.9 jit_solution(17435355348928590986)
XLA Ops:
  7.2 0.7 all-gather.3.cloned.1.call-update
  7.9 1.1 fusion.12
  9.0 1.2 fusion.19
  10.2 2.4 %collective-permute-start = (bf16[2,1,160,384]{3,2,0,1:T(8,128)(2,1)S(1)}, bf16[2,1,160,384]{3,2,0,1:T(8,128)(2,1)S(1)}, u32[]{:S(2)}, u32[]{:S(2)}) collective-permute-start(bf16[2,1,160,384]{3,2,0,1:T(8,128)(2,1)S(1)} %fusion.19), channel_id=1, source_target_pairs={{0,1},{1,2},{2,3},{3,4},{4,5},{5,6},{6,7},{7,8},{8,9},{9,10},{10,1... | collective-permute-start | bytes 737288 | tf_op jit(solution)/shard_map/ppermute | solution.py:66
  12.6 1.1 collective-permute-done
  13.8 0.7 collective-permute-start.1
  14.5 0.7 pad_dynamic-slice_fusion
  15.3 0.3 select_maximum_fusion
  15.6 0.3 fusion.8
  15.9 0.3 pad_maximum_fusion.1
  16.2 3.1 %copy.13 = bf16[3,2,3,162,384]{4,1,3,2,0:T(2,128)(2,1)} copy(bf16[3,2,3,162,384]{4,3,1,2,0:T(8,128)(2,1)S(1)} %pad_maximum_fusion.1) | data formatting | bytes 4478976 | tf_op jit(solution)/shard_map/stack | solution.py:71
  19.3 4.6 %collective-permute-start.2 = (bf16[3,2,3,162,384]{4,1,3,2,0:T(2,128)(2,1)}, bf16[3,2,3,162,384]{4,1,3,2,0:T(2,128)(2,1)}, u32[]{:S(2)}, u32[]{:S(2)}) collective-permute-start(bf16[3,2,3,162,384]{4,1,3,2,0:T(2,128)(2,1)} %copy.13), channel_id=1, source_target_pairs={{0,1},{1,0},{2,3},{3,2},{4,5},{5,4},{6,7},{7,6},{8,9},{9,8},{10,11... | collective-permute-start | bytes 6718472 | tf_op jit(solution)/shard_map/ppermute | solution.py:81
  24.0 4.2 %collective-permute-done.2 = bf16[3,2,3,162,384]{4,1,3,2,0:T(2,128)(2,1)} collective-permute-done((bf16[3,2,3,162,384]{4,1,3,2,0:T(2,128)(2,1)}, bf16[3,2,3,162,384]{4,1,3,2,0:T(2,128)(2,1)}, u32[]{:S(2)}, u32[]{:S(2)}) %collective-permute-start.2) | collective-permute-done | bytes 2239520 | tf_op jit(solution)/shard_map/ppermute | solution.py:81
  28.2 1.9 %copy.14 = bf16[3,2,3,162,384]{4,3,1,2,0:T(8,128)(2,1)S(1)} copy(bf16[3,2,3,162,384]{4,1,3,2,0:T(2,128)(2,1)} %collective-permute-done.2) | data formatting | bytes 4478976 | tf_op jit(solution)/shard_map/ppermute | solution.py:81
  30.1 2.8 %pad_maximum_fusion = bf16[3,4,3,162,384]{4,3,1,2,0:T(8,128)(2,1)} fusion(bf16[3,2,3,162,384]{4,3,1,2,0:T(8,128)(2,1)S(1)} %copy.14, bf16[1,2,3,162,384]{4,3,1,2,0:T(8,128)(2,1)S(1)} %get-tuple-element.10, bf16[1,2,3,162,384]{4,3,1,2,0:T(8,128)(2,1)S(1)} %get-tuple-element.9, bf16[1,2,3,162,384]{4,3,1,2,0:T(8,128)(2,1)S(1)} %get-tuple-element.8), kind=kLoop, calls=%fused_computation.3 | loop fusion | flops 6718464 | bytes 8957952 | tf_op jit(solution)/shard_map/concatenate | solution.py:82
  32.9 50.1 %all-gather.3.cloned.1.call-done = bf16[192,3,3,3,384]{4,0,3,2,1:T(8,128)(2,1)} async-done(((bf16[24,3,3,3,384]{4,0,3,2,1:T(8,128)(2,1)}), bf16[192,3,3,3,384]{4,0,3,2,1:T(8,128)(2,1)}) %all-gather.3.cloned.1.call-update) | async-done | bytes 3981328 | tf_op jit(solution)/shard_map/all_gather | solution.py:84
  83.0 6.7 %bitcast_multiply_fusion = bf16[384,3,3,3,384]{4,0,3,2,1:T(8,128)(2,1)} fusion(bf16[384]{0:T(512)(128)(2,1)S(1)} %mul.109, bf16[8,24,3,3,3,384]{5,1,0,4,3,2:T(8,128)(2,1)} %bitcast.253), kind=kLoop, calls=%fused_computation | loop fusion | flops 3981312 | bytes 11944704 | tf_op jit(solution)/shard_map/mul | solution.py:86
  89.7 1.6 %fusion.22 = f32[4,160,384]{2,1,0:T(8,128)S(1)} fusion(bf16[3,4,3,162,384]{4,3,1,2,0:T(8,128)(2,1)S(1)} %copy-done.1, bf16[384,3,3,3,384]{4,0,3,2,1:T(8,128)(2,1)} %bitcast_multiply_fusion), kind=kOutput, calls=%fused_computation.95 | convolution fusion | flops 188743680 | bytes 1769472 | tf_op jit(solution)/shard_map/fhwc,cd->fhwd/dot_general | solution.py:91
  91.3 1.8 %convolution_add_fusion.25 = f32[4,160,384]{2,1,0:T(8,128)S(1)} fusion(f32[4,160,384]{2,1,0:T(8,128)S(1)} %fusion.22, bf16[3,4,3,162,384]{4,3,1,2,0:T(8,128)(2,1)S(1)} %copy-done.1, bf16[384,3,3,3,384]{4,0,3,2,1:T(8,128)(2,1)} %bitcast_multiply_fusion), kind=kOutput, calls=%fused_computation.37 | convolution fusion | flops 188989440 | bytes 2752512 | tf_op jit(solution)/shard_map/fhwc,cd->fhwd/dot_general | solution.py:91
  93.1 1.4 %convolution_add_fusion.24 = f32[4,160,384]{2,1,0:T(8,128)S(1)} fusion(f32[4,160,384]{2,1,0:T(8,128)S(1)} %convolution_add_fusion.25, bf16[3,4,3,162,384]{4,3,1,2,0:T(8,128)(2,1)S(1)} %copy-done.1, bf16[384,3,3,3,384]{4,0,3,2,1:T(8,128)(2,1)} %bitcast_multiply_fusion), kind=kOutput, calls=%fused_computation.36 | convolution fusion | flops 188989440 | bytes 2752512 | tf_op jit(solution)/shard_map/fhwc,cd->fhwd/dot_general | solution.py:91
  94.5 1.4 %convolution_add_fusion.23 = f32[4,160,384]{2,1,0:T(8,128)S(1)} fusion(f32[4,160,384]{2,1,0:T(8,128)S(1)} %convolution_add_fusion.24, bf16[3,4,3,162,384]{4,3,1,2,0:T(8,128)(2,1)S(1)} %copy-done.1, bf16[384,3,3,3,384]{4,0,3,2,1:T(8,128)(2,1)} %bitcast_multiply_fusion), kind=kOutput, calls=%fused_computation.35 | convolution fusion | flops 188989440 | bytes 2752512 | tf_op jit(solution)/shard_map/fhwc,cd->fhwd/dot_general | solution.py:91
  96.0 0.5 convolution_add_fusion.22
  96.4 0.5 convolution_add_fusion.21
  96.9 0.5 convolution_add_fusion.20
  97.3 0.5 convolution_add_fusion.19
  97.8 0.5 convolution_add_fusion.18
  98.3 0.5 convolution_add_fusion.17
  98.7 0.5 convolution_add_fusion.16
  99.2 0.5 convolution_add_fusion.15
  99.7 0.5 convolution_add_fusion.14
  100.1 0.5 convolution_add_fusion.13
  100.6 0.5 convolution_add_fusion.12
  101.0 0.5 convolution_add_fusion.11
  101.5 0.5 convolution_add_fusion.10
  102.0 0.5 convolution_add_fusion.9
  102.4 0.5 convolution_add_fusion.8
  102.9 0.5 convolution_add_fusion.7
  103.4 0.5 convolution_add_fusion.6
  103.8 0.5 convolution_add_fusion.5
  104.3 0.5 convolution_add_fusion.4
  104.7 0.5 convolution_add_fusion.3
  105.2 0.5 convolution_add_fusion.2
  105.7 0.5 convolution_add_fusion.1
  106.2 0.5 convolution_add_fusion
  106.7 1.9 %collective-permute-done.3 = f32[2,1,160,384]{3,2,0,1:T(8,128)S(1)} collective-permute-done((f32[2,1,160,384]{3,2,0,1:T(8,128)S(1)}, f32[2,1,160,384]{3,2,0,1:T(8,128)S(1)}, u32[]{:S(2)}, u32[]{:S(2)}) %collective-permute-start.3) | collective-permute-done | bytes 491552 | tf_op jit(solution)/shard_map/ppermute | solution.py:97
  108.8 0.6 convolution_convert_fusion
  109.4 0.3 fusion.40
  109.8 1.2 %fusion.5 = bf16[2,1,160,384]{3,2,1,0:T(8,128)(2,1)} fusion(bf16[384,384]{1,0:T(8,128)(2,1)S(1)} %copy-done.6, bf16[2,160,1152]{2,1,0:T(8,128)(2,1)S(1)} %convolution_convert_fusion, f32[2,160]{1,0:T(2,128)S(1)} %fusion.24, f32[2,160,160]{1,2,0:T(8,128)S(1)} %get-tuple-element.14, f32[2,160]{1,0:T(2,128)S(1)} %broadcast_maximum_fusion), kind=kOutput, calls=%fused_computation.42 | convolution fusion | flops 134164480 | bytes 1118208 | tf_op jit(solution)/shard_map/fpc,cd->fpd/dot_general | solution.py:119
  (28 shorter events, 0.8 us)
Async XLA Ops:
  7.2 101.6 %copy-start = (bf16[384,1152]{1,0:T(8,128)(2,1)S(1)}, bf16[384,1152]{1,0:T(8,128)(2,1)}, u32[]{:S(2)}) copy-start(bf16[384,1152]{1,0:T(8,128)(2,1)} %param.12) | copy-start | bytes 2654212
  7.2 75.9 %all-gather.3.cloned.1.call-start = ((), (), s32[]{:S(2)}) async-start(), calls=%async_computation | async-start | bytes 4478976 | tf_op jit(solution)/shard_map/all_gather | solution.py:84
  10.2 3.5 %collective-permute-start = (bf16[2,1,160,384]{3,2,0,1:T(8,128)(2,1)S(1)}, bf16[2,1,160,384]{3,2,0,1:T(8,128)(2,1)S(1)}, u32[]{:S(2)}, u32[]{:S(2)}) collective-permute-start(bf16[2,1,160,384]{3,2,0,1:T(8,128)(2,1)S(1)} %fusion.19), channel_id=1, source_target_pairs={{0,1},{1,2},{2,3},{3,4},{4,5},{5,6},{6,7},{7,8},{8,9},{9,10},{10,1... | collective-permute-start | bytes 737288 | tf_op jit(solution)/shard_map/ppermute | solution.py:66
  13.8 1.5 %collective-permute-start.1 = (bf16[4,1,160,384]{3,2,0,1:T(8,128)(2,1)S(1)}, bf16[4,1,160,384]{3,2,0,1:T(8,128)(2,1)S(1)}, u32[]{:S(2)}, u32[]{:S(2)}) collective-permute-start(bf16[4,1,160,384]{3,2,0,1:T(8,128)(2,1)S(1)} %pad_maximum_fusion.2), channel_id=1, source_target_pairs={} | collective-permute-start | bytes 1474568 | tf_op jit(solution)/shard_map/ppermute | solution.py:27
  19.3 8.9 %collective-permute-start.2 = (bf16[3,2,3,162,384]{4,1,3,2,0:T(2,128)(2,1)}, bf16[3,2,3,162,384]{4,1,3,2,0:T(2,128)(2,1)}, u32[]{:S(2)}, u32[]{:S(2)}) collective-permute-start(bf16[3,2,3,162,384]{4,1,3,2,0:T(2,128)(2,1)} %copy.13), channel_id=1, source_target_pairs={{0,1},{1,0},{2,3},{3,2},{4,5},{5,4},{6,7},{7,6},{8,9},{9,8},{10,11... | collective-permute-start | bytes 6718472 | tf_op jit(solution)/shard_map/ppermute | solution.py:81
  83.0 6.7 %copy-start.1 = (bf16[3,4,3,162,384]{4,3,1,2,0:T(8,128)(2,1)S(1)}, bf16[3,4,3,162,384]{4,3,1,2,0:T(8,128)(2,1)}, u32[]{:S(2)}) copy-start(bf16[3,4,3,162,384]{4,3,1,2,0:T(8,128)(2,1)} %pad_maximum_fusion) | copy-start | bytes 13436932
  89.7 6.2 %copy-start.2 = (bf16[384,3,3,3,384]{4,0,3,2,1:T(8,128)(2,1)S(1)}, bf16[384,3,3,3,384]{4,0,3,2,1:T(8,128)(2,1)}, u32[]{:S(2)}) copy-start(bf16[384,3,3,3,384]{4,0,3,2,1:T(8,128)(2,1)} %bitcast_multiply_fusion) | copy-start | bytes 23887876
  105.2 3.4 %copy-start.3 = (bf16[2,1,160,384]{3,2,1,0:T(8,128)(2,1)S(1)}, bf16[2,1,160,384]{3,2,1,0:T(8,128)(2,1)}, u32[]{:S(2)}) copy-start(bf16[2,1,160,384]{3,2,1,0:T(8,128)(2,1)} %param.7) | copy-start | bytes 737284
  105.7 3.1 %copy-start.5 = (f32[384]{0:T(512)S(1)}, f32[384]{0:T(512)}, u32[]{:S(2)}) copy-start(f32[384]{0:T(512)} %param.11) | copy-start | bytes 4612
  106.1 3.6 %copy-start.6 = (bf16[384,384]{1,0:T(8,128)(2,1)S(1)}, bf16[384,384]{1,0:T(8,128)(2,1)}, u32[]{:S(2)}) copy-start(bf16[384,384]{1,0:T(8,128)(2,1)} %param.13) | copy-start | bytes 884740
  106.7 1.9 %collective-permute-start.3 = (f32[2,1,160,384]{3,2,0,1:T(8,128)S(1)}, f32[2,1,160,384]{3,2,0,1:T(8,128)S(1)}, u32[]{:S(2)}, u32[]{:S(2)}) collective-permute-start(f32[2,1,160,384]{3,2,0,1:T(8,128)S(1)} %slice_bitcast_fusion.1), channel_id=1, source_target_pairs={{0,1},{1,0},{2,3},{3,2},{4,5},{5,4},{6,7},{7,6},{8,9},{9,8},{10,11... | collective-permute-start | bytes 1474568 | tf_op jit(solution)/shard_map/ppermute | solution.py:97
  108.8 2.3 %copy-start.4 = (bf16[2,1,160,384]{3,2,0,1:T(8,128)(2,1)}, bf16[2,1,160,384]{3,2,0,1:T(8,128)(2,1)S(1)}, u32[]{:S(2)}) copy-start(bf16[2,1,160,384]{3,2,0,1:T(8,128)(2,1)S(1)} %get-tuple-element.7) | copy-start | bytes 737284
Sparse Core Ops, SparseCore 0:
  10.3 72.7 all-gather.2

commit v3 on v0

--- a/solution.py
+++ b/solution.py
@@ -72,7 +72,11 @@
         ]
     )
     total = jnp.zeros((depth, height, across, width), jnp.float32)
-    piece = lax.all_gather(conv_weight, "tm", axis=0, tiled=True)
+    halves = conv_weight.reshape((2, conv_weight.shape[0] // 2) + conv_weight.shape[1:])
+    half = lax.dynamic_index_in_dim(halves, lax.axis_index("groups"), 0, keepdims=False)
+    gathered = lax.all_gather(half, ("groups", "tm"), axis=0)
+    gathered = gathered.reshape((2, gathered.shape[0] // 2) + half.shape)
+    piece = jnp.swapaxes(gathered, 0, 1).reshape((width,) + conv_weight.shape[1:])
     for tap_t in range(3):
         for tap_h in range(3):
             for tap_w in range(3):

time: 110 us -> 152 us (1.38)
  local copies, waits for them, and re-layouts: 0.78 us -> 26 us
  waiting for transfers between devices: 70.3 us -> 86.8 us
    all_gather x1, waiting for transfers between devices: 68.5 us -> 85.7 us  [body(): gathered = lax.all_gather(half, ('groups', 'tm'), axis=0)]
    reshape x0 -> x2, local copies, waits for them, and re-layouts: none -> 14.9 us  [the longest x1 13.6 us: body(): jnp.swapaxes(gathered, 0, 1).reshape((width,) + conv_weight.shape[1:])]
    transpose x0 -> x1, local copies, waits for them, and re-layouts: none -> 9.52 us  [body(): jnp.swapaxes(gathered, 0, 1).reshape((width,) + conv_weight.shape[1:])]
  transfers between devices with their start and end apart: 3 -> 3, of which waited for: 2 -> 2; matrix products, arithmetic and copies ran while one was open for 3% -> 2% of each run, Pallas kernels for 0% -> 0%
where the time goes in v3:
time: 152 us; the launch traced here: 151 us
  waiting for transfers between devices  86.8 us (57%)
  local copies, waits for them, and re-layouts  26 us (17%)
  matrix products  17.7 us (12%)
  between operations  14.4 us (9%)
  starting transfers between devices  3.13 us (2%)
  other arithmetic  3.03 us (2%)
    all_gather x1, waiting for transfers between devices, body(): gathered = lax.all_gather(half, ('groups', 'tm'), axis=0)  85.7 us
    dot_general x27, matrix products, body(): jnp.einsum('fhwc,cd->fhwd', window, piece[:, tap_t, tap_h, tap_w, :], pre...  15.6 us
    reshape x1, local copies, waits for them, and re-layouts, body(): jnp.swapaxes(gathered, 0, 1).reshape((width,) + conv_weight.shape[1:])  13.6 us
    transpose x1, local copies, waits for them, and re-layouts, body(): jnp.swapaxes(gathered, 0, 1).reshape((width,) + conv_weight.shape[1:])  9.52 us
  transfers between devices with their start and end apart: 3, of which 2 were waited for; matrix products, arithmetic and copies ran while one was open for 2% of the time, Pallas kernels for 0%

profile of v3, /device:TPU:0, one launch (start us, length us, event | category | flops | bytes accessed | tf_op | source)
XLA Modules:
  0.0 151.0 jit_solution(12528913179161714964)
XLA Ops:
  7.2 0.0 all-gather.2.cloned.1.call-start
  7.2 1.2 reshape.219
  8.5 0.8 constant_dynamic-slice_fusion
  9.3 0.0 all-gather.2.cloned.1.call-update
  9.3 1.1 fusion.15
  10.4 1.2 fusion.22
  11.6 2.4 %collective-permute-start = (bf16[2,1,160,384]{3,2,0,1:T(8,128)(2,1)S(1)}, bf16[2,1,160,384]{3,2,0,1:T(8,128)(2,1)S(1)}, u32[]{:S(2)}, u32[]{:S(2)}) collective-permute-start(bf16[2,1,160,384]{3,2,0,1:T(8,128)(2,1)S(1)} %fusion.22), channel_id=1, source_target_pairs={{0,1},{1,2},{2,3},{3,4},{4,5},{5,6},{6,7},{7,8},{8,9},{9,10},{10,1... | collective-permute-start | bytes 737288 | tf_op jit(solution)/shard_map/ppermute | solution.py:15
  14.0 1.1 collective-permute-done
  15.1 0.1 pad_maximum_fusion
  15.2 0.7 collective-permute-start.1
  15.9 0.7 pad_dynamic-slice_fusion
  16.6 0.1 compare_convert_fusion
  16.7 0.3 select_maximum_fusion
  17.0 0.3 slice_bitcast_fusion
  17.2 85.7 %all-gather.2.cloned.1.call-done = bf16[32,12,3,3,3,384]{5,1,0,4,3,2:T(8,128)(2,1)} async-done(((bf16[1,12,3,3,3,384]{5,1,0,4,3,2:T(8,128)(2,1)}), bf16[32,12,3,3,3,384]{5,1,0,4,3,2:T(8,128)(2,1)}) %all-gather.2.cloned.1.call-update) | async-done | bytes 7962640 | tf_op jit(solution)/shard_map/all_gather | solution.py:77
  103.0 9.5 %copy.14 = bf16[16,2,12,3,3,3,384]{6,2,1,0,5,4,3:T(8,128)(2,1)} copy(bf16[16,2,12,3,3,3,384]{6,2,0,1,5,4,3:T(8,128)(2,1)} %bitcast.259) | data formatting | bytes 15925248 | tf_op jit(solution)/shard_map/transpose | solution.py:79
  112.5 13.6 %reshape.221 = bf16[384,3,3,3,384]{4,0,3,2,1:T(8,128)(2,1)} reshape(bf16[16,2,12,3,3,3,384]{6,2,1,0,5,4,3:T(8,128)(2,1)} %copy.14) | data formatting | bytes 15925248 | tf_op jit(solution)/shard_map/reshape | solution.py:79
  126.1 1.4 fusion.23
  127.5 1.7 %convolution_add_fusion.25 = f32[2,160,384]{2,1,0:T(8,128)S(1)} fusion(f32[2,160,384]{2,1,0:T(8,128)S(1)} %fusion.23, bf16[384,3,3,3,384]{4,0,3,2,1:T(8,128)(2,1)} %reshape.221, bf16[1,2,3,162,384]{4,3,1,2,0:T(8,128)(2,1)S(1)} %get-tuple-element.8), kind=kOutput, calls=%fused_computation.36 | convolution fusion | flops 94494720 | bytes 1523712 | tf_op jit(solution)/shard_map/fhwc,cd->fhwd/dot_general | solution.py:84
  129.2 1.3 convolution_add_fusion.24
  130.5 1.3 convolution_add_fusion.23
  131.8 1.3 convolution_add_fusion.22
  133.2 1.3 convolution_add_fusion.21
  134.5 0.3 convolution_add_fusion.20
  134.8 0.3 convolution_add_fusion.19
  135.2 0.3 convolution_add_fusion.18
  135.5 0.3 convolution_add_fusion.17
  135.9 0.3 convolution_add_fusion.16
  136.2 0.3 convolution_add_fusion.15
  136.5 0.3 convolution_add_fusion.14
  136.9 0.3 convolution_add_fusion.13
  137.2 0.3 convolution_add_fusion.12
  137.6 0.3 convolution_add_fusion.11
  137.9 0.3 convolution_add_fusion.10
  138.3 0.3 convolution_add_fusion.9
  138.6 0.3 convolution_add_fusion.8
  139.0 0.3 convolution_add_fusion.7
  139.3 0.3 convolution_add_fusion.6
  139.7 0.3 convolution_add_fusion.5
  140.0 0.3 convolution_add_fusion.4
  140.4 0.3 convolution_add_fusion.3
  140.7 0.3 convolution_add_fusion.2
  141.1 0.3 convolution_add_fusion.1
  141.4 0.5 fusion.12
  142.0 0.6 convolution_convert_fusion
  142.6 0.3 fusion.40
  142.9 0.1 fusion.25
  142.9 1.2 fusion.8
  (16 shorter events, 0.1 us)
Async XLA Ops:
  7.2 134.8 %copy-start = (bf16[384,1152]{1,0:T(8,128)(2,1)S(1)}, bf16[384,1152]{1,0:T(8,128)(2,1)}, u32[]{:S(2)}) copy-start(bf16[384,1152]{1,0:T(8,128)(2,1)} %param.12) | copy-start | bytes 2654212
  7.2 95.8 %all-gather.2.cloned.1.call-start = ((), (), s32[]{:S(2)}) async-start(), calls=%async_computation | async-start | bytes 10948608 | tf_op jit(solution)/shard_map/all_gather | solution.py:77
  11.6 3.5 %collective-permute-start = (bf16[2,1,160,384]{3,2,0,1:T(8,128)(2,1)S(1)}, bf16[2,1,160,384]{3,2,0,1:T(8,128)(2,1)S(1)}, u32[]{:S(2)}, u32[]{:S(2)}) collective-permute-start(bf16[2,1,160,384]{3,2,0,1:T(8,128)(2,1)S(1)} %fusion.22), channel_id=1, source_target_pairs={{0,1},{1,2},{2,3},{3,4},{4,5},{5,6},{6,7},{7,8},{8,9},{9,10},{10,1... | collective-permute-start | bytes 737288 | tf_op jit(solution)/shard_map/ppermute | solution.py:15
  15.2 1.5 %collective-permute-start.1 = (bf16[4,1,160,384]{3,2,0,1:T(8,128)(2,1)S(1)}, bf16[4,1,160,384]{3,2,0,1:T(8,128)(2,1)S(1)}, u32[]{:S(2)}, u32[]{:S(2)}) collective-permute-start(bf16[4,1,160,384]{3,2,0,1:T(8,128)(2,1)S(1)} %pad_maximum_fusion), channel_id=1, source_target_pairs={} | collective-permute-start | bytes 1474568 | tf_op jit(solution)/shard_map/ppermute | solution.py:26
  126.1 8.4 %copy-start.1 = (bf16[384,3,3,3,384]{4,0,3,2,1:T(8,128)(2,1)S(1)}, bf16[384,3,3,3,384]{4,0,3,2,1:T(8,128)(2,1)}, u32[]{:S(2)}) copy-start(bf16[384,3,3,3,384]{4,0,3,2,1:T(8,128)(2,1)} %reshape.221) | copy-start | bytes 23887876
  137.9 3.5 %copy-start.2 = (bf16[2,1,160,384]{3,2,1,0:T(8,128)(2,1)S(1)}, bf16[2,1,160,384]{3,2,1,0:T(8,128)(2,1)}, u32[]{:S(2)}) copy-start(bf16[2,1,160,384]{3,2,1,0:T(8,128)(2,1)} %param.7) | copy-start | bytes 737284
  138.3 3.7 %copy-start.4 = (f32[384]{0:T(512)S(1)}, f32[384]{0:T(512)}, u32[]{:S(2)}) copy-start(f32[384]{0:T(512)} %param.11) | copy-start | bytes 4612
  139.0 4.0 %copy-start.5 = (bf16[384,384]{1,0:T(8,128)(2,1)S(1)}, bf16[384,384]{1,0:T(8,128)(2,1)}, u32[]{:S(2)}) copy-start(bf16[384,384]{1,0:T(8,128)(2,1)} %param.13) | copy-start | bytes 884740
  141.9 2.3 %copy-start.3 = (bf16[2,1,160,384]{3,2,0,1:T(8,128)(2,1)}, bf16[2,1,160,384]{3,2,0,1:T(8,128)(2,1)S(1)}, u32[]{:S(2)}) copy-start(bf16[2,1,160,384]{3,2,0,1:T(8,128)(2,1)S(1)} %get-tuple-element.12) | copy-start | bytes 737284
Sparse Core Ops, SparseCore 0:
  10.8 92.1 all-gather.1

commit v4 on v0

--- a/solution.py
+++ b/solution.py
@@ -72,7 +72,8 @@
         ]
     )
     total = jnp.zeros((depth, height, across, width), jnp.float32)
-    piece = lax.all_gather(conv_weight, "tm", axis=0, tiled=True)
+    flat_weight = conv_weight.reshape(conv_weight.shape[0], 27 * width)
+    piece = lax.all_gather(flat_weight, "tm", axis=0, tiled=True)
     for tap_t in range(3):
         for tap_h in range(3):
             for tap_w in range(3):
@@ -80,7 +81,7 @@
                 total = total + jnp.einsum(
                     "fhwc,cd->fhwd",
                     window,
-                    piece[:, tap_t, tap_h, tap_w, :],
+                    piece[:, ((tap_t * 3 + tap_h) * 3 + tap_w) * width : ((tap_t * 3 + tap_h) * 3 + tap_w + 1) * width],
                     preferred_element_type=jnp.float32,
                 )
     summed = (inputs + total).astype(jnp.bfloat16)

time: 110 us -> 110 us (level)
  local copies, waits for them, and re-layouts: 0.78 us -> 3.41 us
  waiting for transfers between devices: 70.3 us -> 67.8 us
    all_gather x1, waiting for transfers between devices: 68.5 us -> 66.7 us  [body(): piece = lax.all_gather(flat_weight, 'tm', axis=0, tiled=True)]
    unnamed x12 -> x13, local copies, waits for them, and re-layouts: 0.04 us -> 1.4 us
    reshape x0 -> x1, local copies, waits for them, and re-layouts: none -> 1.27 us  [body(): flat_weight = conv_weight.reshape(conv_weight.shape[0], 27 * width)]
where the time goes in v4:
time: 110 us; the launch traced here: 109 us
  waiting for transfers between devices  67.8 us (62%)
  matrix products  17.8 us (16%)
  between operations  14.4 us (13%)
  local copies, waits for them, and re-layouts  3.41 us (3%)
  starting transfers between devices  3.13 us (3%)
  other arithmetic  3.03 us (3%)
    all_gather x1, waiting for transfers between devices, body(): piece = lax.all_gather(flat_weight, 'tm', axis=0, tiled=True)  66.7 us
    dot_general x27, matrix products, body(): jnp.einsum('fhwc,cd->fhwd', window, piece[:, ((tap_t * 3 + tap_h) * 3 + t...  15.7 us
    ppermute x1, starting transfers between devices, passed_along(): lax.ppermute(value, axis, [(source, source + steps) for source in range(l...  2.41 us
  transfers between devices with their start and end apart: 3, of which 2 were waited for; matrix products, arithmetic and copies ran while one was open for 3% of the time, Pallas kernels for 0%

profile of v4, /device:TPU:0, one launch (start us, length us, event | category | flops | bytes accessed | tf_op | source)
XLA Modules:
  0.0 109.5 jit_solution(11363822072836552671)
XLA Ops:
  7.2 0.0 copy-start
  7.2 0.0 all-gather.2.cloned.1.call-start
  7.2 1.4 %copy.14 = bf16[24,3,3,3,384]{4,3,2,1,0:T(4,128)(2,1)S(1)} copy(bf16[24,3,3,3,384]{4,0,3,2,1:T(8,128)(2,1)} %param.10) | data formatting | bytes 995328 | tf_op args[3]
  8.6 1.3 %reshape.213 = bf16[24,10368]{1,0:T(8,128)(2,1)} reshape(bf16[24,3,3,3,384]{4,3,2,1,0:T(4,128)(2,1)S(1)} %copy.14) | data formatting | bytes 995328 | tf_op jit(solution)/shard_map/reshape | solution.py:75
  9.9 0.0 all-gather.2.cloned.1.call-update
  9.9 1.1 fusion.15
  11.0 1.2 %fusion.22 = bf16[2,1,160,384]{3,2,0,1:T(8,128)(2,1)S(1)} fusion(bf16[2,1,160,384]{3,2,1,0:T(8,128)(2,1)} %param.7, f32[384]{0:T(512)} %param.9, f32[2,160]{1,0:T(2,128)S(1)} %add_rsqrt_fusion.1), kind=kLoop, calls=%fused_computation.63 | loop fusion | flops 983040 | bytes 494336 | tf_op jit(solution)/shard_map/convert_element_type | solution.py:57
  12.2 2.4 %collective-permute-start = (bf16[2,1,160,384]{3,2,0,1:T(8,128)(2,1)S(1)}, bf16[2,1,160,384]{3,2,0,1:T(8,128)(2,1)S(1)}, u32[]{:S(2)}, u32[]{:S(2)}) collective-permute-start(bf16[2,1,160,384]{3,2,0,1:T(8,128)(2,1)S(1)} %fusion.22), channel_id=1, source_target_pairs={{0,1},{1,2},{2,3},{3,4},{4,5},{5,6},{6,7},{7,8},{8,9},{9,10},{10,1... | collective-permute-start | bytes 737288 | tf_op jit(solution)/shard_map/ppermute | solution.py:15
  14.6 1.1 %collective-permute-done = bf16[2,1,160,384]{3,2,0,1:T(8,128)(2,1)S(1)} collective-permute-done((bf16[2,1,160,384]{3,2,0,1:T(8,128)(2,1)S(1)}, bf16[2,1,160,384]{3,2,0,1:T(8,128)(2,1)S(1)}, u32[]{:S(2)}, u32[]{:S(2)}) %collective-permute-start) | collective-permute-done | bytes 245792 | tf_op jit(solution)/shard_map/ppermute | solution.py:15
  15.7 0.1 pad_maximum_fusion
  15.8 0.7 collective-permute-start.1
  16.5 0.7 pad_dynamic-slice_fusion
  17.2 0.1 compare_convert_fusion
  17.3 0.3 select_maximum_fusion
  17.6 0.3 slice_bitcast_fusion
  17.8 66.7 %all-gather.2.cloned.1.call-done = bf16[384,10368]{1,0:T(8,128)(2,1)} async-done(((bf16[24,10368]{1,0:T(8,128)(2,1)}), bf16[384,10368]{1,0:T(8,128)(2,1)}) %all-gather.2.cloned.1.call-update) | async-done | bytes 7962640 | tf_op jit(solution)/shard_map/all_gather | solution.py:76
  84.5 1.4 %fusion.23 = f32[2,160,384]{2,1,0:T(8,128)S(1)} fusion(bf16[384,10368]{1,0:T(8,128)(2,1)} %all-gather.2.cloned.1.call-done, bf16[1,2,3,162,384]{4,3,1,2,0:T(8,128)(2,1)S(1)} %get-tuple-element.8), kind=kOutput, calls=%fused_computation.93 | convolution fusion | flops 94371840 | bytes 1032192 | tf_op jit(solution)/shard_map/fhwc,cd->fhwd/dot_general | solution.py:81
  85.9 1.7 %convolution_add_fusion.25 = f32[2,160,384]{2,1,0:T(8,128)S(1)} fusion(f32[2,160,384]{2,1,0:T(8,128)S(1)} %fusion.23, bf16[384,10368]{1,0:T(8,128)(2,1)} %all-gather.2.cloned.1.call-done, bf16[1,2,3,162,384]{4,3,1,2,0:T(8,128)(2,1)S(1)} %get-tuple-element.8), kind=kOutput, calls=%fused_computation.36 | convolution fusion | flops 94494720 | bytes 1523712 | tf_op jit(solution)/shard_map/fhwc,cd->fhwd/dot_general | solution.py:81
  87.6 1.3 %convolution_add_fusion.24 = f32[2,160,384]{2,1,0:T(8,128)S(1)} fusion(f32[2,160,384]{2,1,0:T(8,128)S(1)} %convolution_add_fusion.25, bf16[384,10368]{1,0:T(8,128)(2,1)} %all-gather.2.cloned.1.call-done, bf16[1,2,3,162,384]{4,3,1,2,0:T(8,128)(2,1)S(1)} %get-tuple-element.8), kind=kOutput, calls=%fused_computation.35 | convolution fusion | flops 94494720 | bytes 1523712 | tf_op jit(solution)/shard_map/fhwc,cd->fhwd/dot_general | solution.py:81
  88.9 1.3 %convolution_add_fusion.23 = f32[2,160,384]{2,1,0:T(8,128)S(1)} fusion(f32[2,160,384]{2,1,0:T(8,128)S(1)} %convolution_add_fusion.24, bf16[384,10368]{1,0:T(8,128)(2,1)} %all-gather.2.cloned.1.call-done, bf16[1,2,3,162,384]{4,3,1,2,0:T(8,128)(2,1)S(1)} %get-tuple-element.8), kind=kOutput, calls=%fused_computation.34 | convolution fusion | flops 94494720 | bytes 1523712 | tf_op jit(solution)/shard_map/fhwc,cd->fhwd/dot_general | solution.py:81
  90.2 1.3 %convolution_add_fusion.22 = f32[2,160,384]{2,1,0:T(8,128)S(1)} fusion(f32[2,160,384]{2,1,0:T(8,128)S(1)} %convolution_add_fusion.23, bf16[384,10368]{1,0:T(8,128)(2,1)} %all-gather.2.cloned.1.call-done, bf16[1,2,3,162,384]{4,3,1,2,0:T(8,128)(2,1)S(1)} %get-tuple-element.8), kind=kOutput, calls=%fused_computation.33 | convolution fusion | flops 94494720 | bytes 1523712 | tf_op jit(solution)/shard_map/fhwc,cd->fhwd/dot_general | solution.py:81
  91.6 1.3 %convolution_add_fusion.21 = f32[2,160,384]{2,1,0:T(8,128)S(1)} fusion(f32[2,160,384]{2,1,0:T(8,128)S(1)} %convolution_add_fusion.22, bf16[384,10368]{1,0:T(8,128)(2,1)} %all-gather.2.cloned.1.call-done, bf16[1,2,3,162,384]{4,3,1,2,0:T(8,128)(2,1)S(1)} %get-tuple-element.8), kind=kOutput, calls=%fused_computation.32 | convolution fusion | flops 94494720 | bytes 1523712 | tf_op jit(solution)/shard_map/fhwc,cd->fhwd/dot_general | solution.py:81
  92.9 0.3 convolution_add_fusion.20
  93.2 0.3 convolution_add_fusion.19
  93.6 0.3 convolution_add_fusion.18
  93.9 0.3 convolution_add_fusion.17
  94.3 0.3 convolution_add_fusion.16
  94.6 0.3 convolution_add_fusion.15
  95.0 0.3 convolution_add_fusion.14
  95.3 0.3 convolution_add_fusion.13
  95.7 0.3 convolution_add_fusion.12
  96.0 0.3 convolution_add_fusion.11
  96.4 0.3 convolution_add_fusion.10
  96.7 0.3 convolution_add_fusion.9
  97.1 0.3 convolution_add_fusion.8
  97.4 0.3 convolution_add_fusion.7
  97.8 0.3 convolution_add_fusion.6
  98.1 0.3 convolution_add_fusion.5
  98.5 0.4 convolution_add_fusion.4
  98.8 0.4 convolution_add_fusion.3
  99.2 0.3 convolution_add_fusion.2
  99.5 0.4 convolution_add_fusion.1
  99.9 0.5 fusion.12
  100.4 0.0 copy-start.3
  100.4 0.6 convolution_convert_fusion
  101.1 0.3 fusion.40
  101.3 0.1 fusion.25
  101.4 1.2 %fusion.8 = bf16[2,1,160,384]{3,2,1,0:T(8,128)(2,1)} fusion(bf16[384,384]{1,0:T(8,128)(2,1)S(1)} %copy-done.5, bf16[2,160,1152]{2,1,0:T(8,128)(2,1)S(1)} %convolution_convert_fusion, f32[2,160]{1,0:T(2,128)S(1)} %fusion.25, f32[2,160,160]{1,2,0:T(8,128)S(1)} %get-tuple-element.14, f32[2,160]{1,0:T(2,128)S(1)} %broadcast_maximum_fusion), kind=kOutput, calls=%fused_computation.42 | convolution fusion | flops 134164480 | bytes 1118208 | tf_op jit(solution)/shard_map/fpc,cd->fpd/dot_general | solution.py:107
  (14 shorter events, 0.0 us)
Async XLA Ops:
  7.2 93.3 %copy-start = (bf16[384,1152]{1,0:T(8,128)(2,1)S(1)}, bf16[384,1152]{1,0:T(8,128)(2,1)}, u32[]{:S(2)}) copy-start(bf16[384,1152]{1,0:T(8,128)(2,1)} %param.12) | copy-start | bytes 2654212
  7.2 77.3 %all-gather.2.cloned.1.call-start = ((), (), s32[]{:S(2)}) async-start(), calls=%async_computation | async-start | bytes 8460288 | tf_op jit(solution)/shard_map/all_gather | solution.py:76
  12.2 3.5 %collective-permute-start = (bf16[2,1,160,384]{3,2,0,1:T(8,128)(2,1)S(1)}, bf16[2,1,160,384]{3,2,0,1:T(8,128)(2,1)S(1)}, u32[]{:S(2)}, u32[]{:S(2)}) collective-permute-start(bf16[2,1,160,384]{3,2,0,1:T(8,128)(2,1)S(1)} %fusion.22), channel_id=1, source_target_pairs={{0,1},{1,2},{2,3},{3,4},{4,5},{5,6},{6,7},{7,8},{8,9},{9,10},{10,1... | collective-permute-start | bytes 737288 | tf_op jit(solution)/shard_map/ppermute | solution.py:15
  15.8 1.5 %collective-permute-start.1 = (bf16[4,1,160,384]{3,2,0,1:T(8,128)(2,1)S(1)}, bf16[4,1,160,384]{3,2,0,1:T(8,128)(2,1)S(1)}, u32[]{:S(2)}, u32[]{:S(2)}) collective-permute-start(bf16[4,1,160,384]{3,2,0,1:T(8,128)(2,1)S(1)} %pad_maximum_fusion), channel_id=1, source_target_pairs={} | collective-permute-start | bytes 1474568 | tf_op jit(solution)/shard_map/ppermute | solution.py:26
  84.5 8.4 %copy-start.1 = (bf16[384,10368]{1,0:T(8,128)(2,1)S(1)}, bf16[384,10368]{1,0:T(8,128)(2,1)}, u32[]{:S(2)}) copy-start(bf16[384,10368]{1,0:T(8,128)(2,1)} %all-gather.2.cloned.1.call-done) | copy-start | bytes 23887876
  96.4 3.6 %copy-start.2 = (bf16[2,1,160,384]{3,2,1,0:T(8,128)(2,1)S(1)}, bf16[2,1,160,384]{3,2,1,0:T(8,128)(2,1)}, u32[]{:S(2)}) copy-start(bf16[2,1,160,384]{3,2,1,0:T(8,128)(2,1)} %param.7) | copy-start | bytes 737284
  96.7 3.7 %copy-start.4 = (f32[384]{0:T(512)S(1)}, f32[384]{0:T(512)}, u32[]{:S(2)}) copy-start(f32[384]{0:T(512)} %param.11) | copy-start | bytes 4612
  97.4 4.0 %copy-start.5 = (bf16[384,384]{1,0:T(8,128)(2,1)S(1)}, bf16[384,384]{1,0:T(8,128)(2,1)}, u32[]{:S(2)}) copy-start(bf16[384,384]{1,0:T(8,128)(2,1)} %param.13) | copy-start | bytes 884740
  100.4 2.2 %copy-start.3 = (bf16[2,1,160,384]{3,2,0,1:T(8,128)(2,1)}, bf16[2,1,160,384]{3,2,0,1:T(8,128)(2,1)S(1)}, u32[]{:S(2)}) copy-start(bf16[2,1,160,384]{3,2,0,1:T(8,128)(2,1)S(1)} %get-tuple-element.12) | copy-start | bytes 737284
Sparse Core Ops, SparseCore 0:
  10.2 74.2 all-gather.1

commit v5 on v0

--- a/solution.py
+++ b/solution.py
@@ -71,18 +71,22 @@
             for tap_t in range(3)
         ]
     )
-    total = jnp.zeros((depth, height, across, width), jnp.float32)
     piece = lax.all_gather(conv_weight, "tm", axis=0, tiled=True)
-    for tap_t in range(3):
-        for tap_h in range(3):
-            for tap_w in range(3):
-                window = masked[tap_t, :, tap_h : tap_h + height, tap_w : tap_w + across, :]
-                total = total + jnp.einsum(
-                    "fhwc,cd->fhwd",
-                    window,
-                    piece[:, tap_t, tap_h, tap_w, :],
-                    preferred_element_type=jnp.float32,
-                )
+    windows = jnp.stack(
+        [
+            masked[tap_t, :, tap_h : tap_h + height, tap_w : tap_w + across, :]
+            for tap_t in range(3)
+            for tap_h in range(3)
+            for tap_w in range(3)
+        ],
+        axis=3,
+    )
+    total = jnp.einsum(
+        "fhwtc,ctd->fhwd",
+        windows,
+        piece.reshape(width, 27, width),
+        preferred_element_type=jnp.float32,
+    )
     summed = (inputs + total).astype(jnp.bfloat16)
     normed = normalize(summed.astype(jnp.float32), attn_gain).astype(jnp.bfloat16)
     flat = normed.reshape(depth, height * across, width)

time: 110 us -> 103 us (0.936)
  local copies, waits for them, and re-layouts: 0.78 us -> 21.1 us
  waiting for transfers between devices: 70.3 us -> 50 us
  matrix products: 17.7 us -> 11 us
    all_gather x1, waiting for transfers between devices: 68.5 us -> 48.2 us  [body(): piece = lax.all_gather(conv_weight, 'tm', axis=0, tiled=True)]
    unnamed x12 -> x36, local copies, waits for them, and re-layouts: 0.04 us -> 19.6 us
    dot_general x27 -> x1, matrix products: 15.6 us -> 8.94 us  [body(): jnp.einsum('fhwtc,ctd->fhwd', windows, piece.reshape(width, 27, width), p...]
  transfers between devices with their start and end apart: 3 -> 3, of which waited for: 2 -> 2; matrix products, arithmetic and copies ran while one was open for 3% -> 23% of each run, Pallas kernels for 0% -> 0%
where the time goes in v5:
time: 103 us; the launch traced here: 102 us
  waiting for transfers between devices  50 us (49%)
  local copies, waits for them, and re-layouts  21.1 us (20%)
  between operations  14.2 us (14%)
  matrix products  11 us (11%)
  starting transfers between devices  3.13 us (3%)
  other arithmetic  3.03 us (3%)
    all_gather x1, waiting for transfers between devices, body(): piece = lax.all_gather(conv_weight, 'tm', axis=0, tiled=True)  48.2 us
    unnamed x36, local copies, waits for them, and re-layouts  19.6 us
    dot_general x1, matrix products, body(): jnp.einsum('fhwtc,ctd->fhwd', windows, piece.reshape(width, 27, width), p...  8.94 us
    ppermute x1, starting transfers between devices, passed_along(): lax.ppermute(value, axis, [(source, source + steps) for source in range(l...  2.41 us
  transfers between devices with their start and end apart: 3, of which 2 were waited for; matrix products, arithmetic and copies ran while one was open for 23% of the time, Pallas kernels for 0%

profile of v5, /device:TPU:0, one launch (start us, length us, event | category | flops | bytes accessed | tf_op | source)
XLA Modules:
  0.0 102.4 jit_solution(5550718627005763535)
XLA Ops:
  7.2 0.0 copy-start
  7.2 0.0 all-gather.2.cloned.1.call-start
  7.2 0.7 all-gather.2.cloned.1.call-update
  7.9 1.1 %fusion.23 = f32[2,160]{1,0:T(2,128)S(1)} fusion(bf16[2,1,160,384]{3,2,1,0:T(8,128)(2,1)} %param.7), kind=kLoop, calls=%fused_computation.32 | loop fusion | flops 368320 | bytes 247040 | tf_op jit(solution)/shard_map/reduce_sum | solution.py:36
  9.0 1.2 %fusion.30 = bf16[2,1,160,384]{3,2,0,1:T(8,128)(2,1)S(1)} fusion(bf16[2,1,160,384]{3,2,1,0:T(8,128)(2,1)} %param.7, f32[384]{0:T(512)} %param.9, f32[2,160]{1,0:T(2,128)S(1)} %add_rsqrt_fusion.1), kind=kLoop, calls=%fused_computation.39 | loop fusion | flops 983040 | bytes 494336 | tf_op jit(solution)/shard_map/convert_element_type | solution.py:57
  10.2 2.4 %collective-permute-start = (bf16[2,1,160,384]{3,2,0,1:T(8,128)(2,1)S(1)}, bf16[2,1,160,384]{3,2,0,1:T(8,128)(2,1)S(1)}, u32[]{:S(2)}, u32[]{:S(2)}) collective-permute-start(bf16[2,1,160,384]{3,2,0,1:T(8,128)(2,1)S(1)} %fusion.30), channel_id=1, source_target_pairs={{0,1},{1,2},{2,3},{3,4},{4,5},{5,6},{6,7},{7,8},{8,9},{9,10},{10,1... | collective-permute-start | bytes 737288 | tf_op jit(solution)/shard_map/ppermute | solution.py:15
  12.6 1.1 %collective-permute-done = bf16[2,1,160,384]{3,2,0,1:T(8,128)(2,1)S(1)} collective-permute-done((bf16[2,1,160,384]{3,2,0,1:T(8,128)(2,1)S(1)}, bf16[2,1,160,384]{3,2,0,1:T(8,128)(2,1)S(1)}, u32[]{:S(2)}, u32[]{:S(2)}) %collective-permute-start) | collective-permute-done | bytes 245792 | tf_op jit(solution)/shard_map/ppermute | solution.py:15
  13.7 0.1 pad_maximum_fusion
  13.8 0.7 collective-permute-start.1
  14.5 0.7 pad_dynamic-slice_fusion
  15.2 0.1 compare_convert_fusion
  15.3 0.3 select_maximum_fusion
  15.6 0.3 slice_bitcast_fusion
  15.9 0.0 copy-start.1
  15.9 0.7 fusion.66
  16.6 0.8 fusion.65
  17.4 0.8 fusion.64
  18.1 0.7 fusion.63
  18.8 0.8 fusion.62
  19.6 0.8 fusion.61
  20.4 0.7 fusion.60
  21.1 0.8 fusion.59
  21.9 0.8 fusion.58
  22.6 0.7 fusion.57
  23.3 0.8 fusion.56
  24.1 0.8 fusion.55
  24.9 0.7 fusion.54
  25.6 0.8 fusion.53
  26.4 0.8 fusion.52
  27.1 0.7 fusion.51
  27.9 0.8 fusion.50
  28.7 0.8 fusion.49
  29.4 0.7 fusion.48
  30.2 0.8 fusion.47
  30.9 0.8 fusion.46
  31.7 0.7 fusion.45
  32.4 0.7 fusion.44
  33.2 0.8 fusion.43
  33.9 0.7 fusion.42
  34.7 0.8 fusion.41
  35.4 0.8 fusion.40
  36.2 48.2 %all-gather.2.cloned.1.call-done = bf16[384,3,3,3,384]{4,0,3,2,1:T(8,128)(2,1)} async-done(((bf16[24,3,3,3,384]{4,0,3,2,1:T(8,128)(2,1)}), bf16[384,3,3,3,384]{4,0,3,2,1:T(8,128)(2,1)}) %all-gather.2.cloned.1.call-update) | async-done | bytes 7962640 | tf_op jit(solution)/shard_map/all_gather | solution.py:74
  84.4 8.9 %fusion.20 = (f32[2,160]{1,0:T(2,128)S(1)}, bf16[2,1,160,384]{3,2,0,1:T(8,128)(2,1)S(1)}) fusion(bf16[384,27,384,1]{2,0,1,3:T(8,128)(2,1)} %bitcast.208, bf16[2,1,160,27,384]{4,2,3,0,1:T(8,128)(2,1)} %fusion.40, bf16[2,1,160,384]{3,2,1,0:T(8,128)(2,1)S(1)} %copy-done.1), kind=kOutput, calls=%fused_computation.29 | convolution fusion | flops 2548776704 | bytes 15090944 | tf_op jit(solution)/shard_map/fhwtc,ctd->fhwd/dot_general | solution.py:84
  93.3 0.0 copy-start.2
  93.4 0.6 convolution_convert_fusion
  94.0 0.3 fusion.74
  94.3 0.1 fusion.32
  94.3 1.2 %fusion.16 = bf16[2,1,160,384]{3,2,1,0:T(8,128)(2,1)} fusion(bf16[384,384]{1,0:T(8,128)(2,1)S(1)} %copy-done.4, bf16[2,160,1152]{2,1,0:T(8,128)(2,1)S(1)} %convolution_convert_fusion, f32[2,160]{1,0:T(2,128)S(1)} %fusion.32, f32[2,160,160]{1,2,0:T(8,128)S(1)} %get-tuple-element.12, f32[2,160]{1,0:T(2,128)S(1)} %broadcast_maximum_fusion), kind=kOutput, calls=%fused_computation.18 | convolution fusion | flops 134164480 | bytes 1118208 | tf_op jit(solution)/shard_map/fpc,cd->fpd/dot_general | solution.py:110
  (11 shorter events, 0.0 us)
Async XLA Ops:
  7.2 86.2 %copy-start = (bf16[384,1152]{1,0:T(8,128)(2,1)S(1)}, bf16[384,1152]{1,0:T(8,128)(2,1)}, u32[]{:S(2)}) copy-start(bf16[384,1152]{1,0:T(8,128)(2,1)} %param.12) | copy-start | bytes 2654212
  7.2 77.2 %all-gather.2.cloned.1.call-start = ((), (), s32[]{:S(2)}) async-start(), calls=%async_computation | async-start | bytes 8460288 | tf_op jit(solution)/shard_map/all_gather | solution.py:74
  10.2 3.5 %collective-permute-start = (bf16[2,1,160,384]{3,2,0,1:T(8,128)(2,1)S(1)}, bf16[2,1,160,384]{3,2,0,1:T(8,128)(2,1)S(1)}, u32[]{:S(2)}, u32[]{:S(2)}) collective-permute-start(bf16[2,1,160,384]{3,2,0,1:T(8,128)(2,1)S(1)} %fusion.30), channel_id=1, source_target_pairs={{0,1},{1,2},{2,3},{3,4},{4,5},{5,6},{6,7},{7,8},{8,9},{9,10},{10,1... | collective-permute-start | bytes 737288 | tf_op jit(solution)/shard_map/ppermute | solution.py:15
  13.8 1.5 %collective-permute-start.1 = (bf16[4,1,160,384]{3,2,0,1:T(8,128)(2,1)S(1)}, bf16[4,1,160,384]{3,2,0,1:T(8,128)(2,1)S(1)}, u32[]{:S(2)}, u32[]{:S(2)}) collective-permute-start(bf16[4,1,160,384]{3,2,0,1:T(8,128)(2,1)S(1)} %pad_maximum_fusion), channel_id=1, source_target_pairs={} | collective-permute-start | bytes 1474568 | tf_op jit(solution)/shard_map/ppermute | solution.py:26
  15.9 68.5 %copy-start.1 = (bf16[2,1,160,384]{3,2,1,0:T(8,128)(2,1)S(1)}, bf16[2,1,160,384]{3,2,1,0:T(8,128)(2,1)}, u32[]{:S(2)}) copy-start(bf16[2,1,160,384]{3,2,1,0:T(8,128)(2,1)} %param.7) | copy-start | bytes 737284
  84.4 9.0 %copy-start.3 = (f32[384]{0:T(512)S(1)}, f32[384]{0:T(512)}, u32[]{:S(2)}) copy-start(f32[384]{0:T(512)} %param.11) | copy-start | bytes 4612
  84.4 10.0 %copy-start.4 = (bf16[384,384]{1,0:T(8,128)(2,1)S(1)}, bf16[384,384]{1,0:T(8,128)(2,1)}, u32[]{:S(2)}) copy-start(bf16[384,384]{1,0:T(8,128)(2,1)} %param.13) | copy-start | bytes 884740
  93.3 2.2 %copy-start.2 = (bf16[2,1,160,384]{3,2,0,1:T(8,128)(2,1)}, bf16[2,1,160,384]{3,2,0,1:T(8,128)(2,1)S(1)}, u32[]{:S(2)}) copy-start(bf16[2,1,160,384]{3,2,0,1:T(8,128)(2,1)S(1)} %get-tuple-element.10) | copy-start | bytes 737284
Sparse Core Ops, SparseCore 0:
  10.2 74.1 all-gather.1
